TPU v7x, 128 devices: a whole 4x4x4 slice. The times are simulated.
128 devices in a mesh: tm: 32 (over z, x_lo, y), head: 4 (over x_hi, core).
Axes of the slice: x: 4 (x_hi: 2, x_lo: 2; x = x_hi * 2 + x_lo), y: 4, z: 4, core: 2. Of those that a mesh axis runs over, the one named last changes fastest.
Arguments:
- queries: bfloat16 [32768, 1024], P('tm', 'head'), may hold values from -8 to 8
- keys: bfloat16 [32768, 1024], P('tm', 'head'), may hold values from -8 to 8
- values: bfloat16 [32768, 1024], P('tm', 'head'), may hold values from -6 to 6
- out_weight: bfloat16 [1024, 1024], P('head'), may hold values from -0.1875 to 0.1875
- grad_output: bfloat16 [32768, 1024], P('tm'), may hold values from -6 to 6
- tile_lists: int32 [256, 5], P('tm'), may hold values from -1 to 255, as said below
Outputs:
- output: bfloat16 [32768, 1024], P('tm', 'head')
- grad_queries: bfloat16 [32768, 1024], P('tm', 'head')
- grad_keys: bfloat16 [32768, 1024], P('tm', 'head')
- grad_values: bfloat16 [32768, 1024], P('tm', 'head')
- grad_weight: float32 [1024, 1024], P('head', 'tm')
Inputs may be any that keep to these rules, and one draw needn't show every extreme that they name: `tile_lists`: the row of query tile b lists distinct key tiles t of b's recording session with b - 4 <= t <= b in falling order, the first entry b itself, then -1 in unused slots; the first tile of every stretch but the first lists the tile before it; in every draw some row uses all 5 slots.
All inputs are finite; a program needn't handle non-finite values.
Results may differ from a plain program's by a relative error of at most 0.0095.
Values may be sent and summed in bfloat16 or wider, within the bound.
No kernel may reach another device: no remote copies, remote signals or barrier semaphores. Data moves between devices by JAX's collectives and lax.ppermute only.
A program may use at most 128 MiB of HBM per device.

v0:
```python
import jax
import jax.numpy as jnp
from jax import lax
from jax.sharding import PartitionSpec as P

HD = 64
QB = 128


def from_behind(x, axis, by):
    devices = lax.axis_size(axis)
    pairs = [(i, i + by) for i in range(devices) if 0 <= i + by < devices]
    return lax.ppermute(x, axis, pairs)


def tile_allow(tile_rows, first_tile, span_tiles):
    tile_span = jnp.arange(2 * span_tiles, dtype=jnp.int32)
    wanted = first_tile[:, None] + tile_span[None, :]
    matched = (tile_rows[:, :, :, None] == wanted[:, None, None, :]) & (
        tile_rows[:, :, :, None] >= 0
    )
    return jnp.any(matched, axis=2)


def group_mask(allow_tiles, first_row, group_rows, span_rows):
    key_width = span_rows + group_rows
    tile_block = allow_tiles[
        :,
        first_row // QB : (first_row + group_rows) // QB,
        first_row // QB : (first_row + key_width) // QB,
    ]
    tile_block = jnp.repeat(jnp.repeat(tile_block, QB, axis=1), QB, axis=2)
    causal = jnp.arange(key_width)[None, :] <= jnp.arange(group_rows)[:, None] + span_rows
    return tile_block & causal[None]


def window_logits(q_group, k_group, allowed, score_scale):
    logits = (
        jnp.einsum("bqhd,bkhd->bhqk", q_group, k_group, preferred_element_type=jnp.float32)
        * score_scale
    )
    return jnp.where(allowed[:, None], logits, -1e30)


def on_device(queries, keys, values, out_weight, grad_output, tile_lists):
    feature_width = queries.shape[1]
    local_heads = feature_width // HD
    span_rows = queries.shape[0] // 2
    span_tiles = span_rows // QB
    group_rows = 256
    group_count = span_rows // group_rows
    score_scale = HD ** (-0.5)
    tm_count = lax.axis_size("tm")
    tm_index = lax.axis_index("tm")
    is_last = tm_index == tm_count - 1
    token_total = tm_count * queries.shape[0]
    q_half = queries.reshape(2, span_rows, local_heads, HD)
    k_half = keys.reshape(2, span_rows, local_heads, HD)
    v_half = values.reshape(2, span_rows, local_heads, HD)
    k_before_low, v_before_low = from_behind((k_half[0], v_half[0]), "tm", 1)
    k_recv_high, v_recv_high = from_behind((k_half[1], v_half[1]), "tm", -1)
    k_before_high = jnp.where(is_last, k_half[0], k_recv_high)
    v_before_high = jnp.where(is_last, v_half[0], v_recv_high)
    k_window = jnp.stack(
        [
            jnp.concatenate([k_before_low, k_half[0]], axis=0),
            jnp.concatenate([k_before_high, k_half[1]], axis=0),
        ]
    )
    v_window = jnp.stack(
        [
            jnp.concatenate([v_before_low, v_half[0]], axis=0),
            jnp.concatenate([v_before_high, v_half[1]], axis=0),
        ]
    )
    piece_ids = jnp.stack([tm_index, 2 * tm_count - 1 - tm_index])
    first_tile = (piece_ids - 1) * span_tiles
    allow_tiles = tile_allow(tile_lists.reshape(2, span_tiles, -1), first_tile, span_tiles)
    out_parts = []
    log_parts = []
    masks = []
    for block_index in range(group_count):
        first_row = block_index * group_rows
        allowed = group_mask(allow_tiles, first_row, group_rows, span_rows)
        masks.append(allowed)
        q_group = q_half[:, first_row : first_row + group_rows]
        k_group = k_window[:, first_row : first_row + span_rows + group_rows]
        v_group = v_window[:, first_row : first_row + span_rows + group_rows]
        logits = window_logits(q_group, k_group, allowed, score_scale)
        row_max = jnp.max(logits, axis=-1, keepdims=True)
        probability = jnp.exp(logits - row_max)
        row_total = jnp.sum(probability, axis=-1)
        mixture = jnp.einsum(
            "bhqk,bkhd->bqhd",
            probability.astype(jnp.bfloat16),
            v_group,
            preferred_element_type=jnp.float32,
        )
        total_rows = jnp.transpose(row_total, (0, 2, 1))[..., None]
        out_parts.append((mixture / total_rows).astype(jnp.bfloat16))
        log_parts.append(row_max[..., 0] + jnp.log(row_total))
    attended = jnp.concatenate(out_parts, axis=1)
    attended_flat = attended.reshape(2 * span_rows, feature_width)
    partial_value = jnp.dot(attended_flat, out_weight, preferred_element_type=jnp.float32)
    summed = lax.psum_scatter(partial_value, "head", scatter_dimension=1, tiled=True)
    output = summed.astype(jnp.bfloat16)
    grad_attn = lax.dot_general(
        grad_output, out_weight, (((1,), (1,)), ((), ())), preferred_element_type=jnp.float32
    ).astype(jnp.bfloat16)
    weight_term = lax.dot_general(
        attended_flat, grad_output, (((0,), (0,)), ((), ())), preferred_element_type=jnp.float32
    )
    grad_weight = lax.psum_scatter(
        weight_term, "tm", scatter_dimension=1, tiled=True
    ) * token_total ** (-0.5)
    g_half = grad_attn.reshape(2, span_rows, local_heads, HD)
    row_delta = jnp.sum(g_half.astype(jnp.float32) * attended.astype(jnp.float32), axis=-1)
    dk_window = jnp.zeros((2, 2 * span_rows, local_heads, HD), jnp.float32)
    dv_window = jnp.zeros((2, 2 * span_rows, local_heads, HD), jnp.float32)
    dq_parts = []
    for block_index in range(group_count):
        first_row = block_index * group_rows
        last_key = first_row + span_rows + group_rows
        q_group = q_half[:, first_row : first_row + group_rows]
        k_group = k_window[:, first_row:last_key]
        v_group = v_window[:, first_row:last_key]
        g_group = g_half[:, first_row : first_row + group_rows]
        logits = window_logits(q_group, k_group, masks[block_index], score_scale)
        back_prob = jnp.exp(logits - log_parts[block_index][..., None])
        back_round = back_prob.astype(jnp.bfloat16)
        dv_part = jnp.einsum(
            "bhqk,bqhd->bkhd", back_round, g_group, preferred_element_type=jnp.float32
        )
        dprob = jnp.einsum("bqhd,bkhd->bhqk", g_group, v_group, preferred_element_type=jnp.float32)
        delta_group = jnp.transpose(row_delta[:, first_row : first_row + group_rows], (0, 2, 1))[
            ..., None
        ]
        dscore_round = (back_prob * (dprob - delta_group)).astype(jnp.bfloat16)
        dq_parts.append(
            jnp.einsum("bhqk,bkhd->bqhd", dscore_round, k_group, preferred_element_type=jnp.float32)
            * score_scale
        )
        dk_part = (
            jnp.einsum("bhqk,bqhd->bkhd", dscore_round, q_group, preferred_element_type=jnp.float32)
            * score_scale
        )
        dk_window = dk_window.at[:, first_row:last_key].add(dk_part)
        dv_window = dv_window.at[:, first_row:last_key].add(dv_part)
    dk_down, dv_down = from_behind((dk_window[0, :span_rows], dv_window[0, :span_rows]), "tm", -1)
    dk_up, dv_up = from_behind((dk_window[1, :span_rows], dv_window[1, :span_rows]), "tm", 1)
    dk_low = dk_window[0, span_rows:] + jnp.where(is_last, dk_window[1, :span_rows], dk_down)
    dv_low = dv_window[0, span_rows:] + jnp.where(is_last, dv_window[1, :span_rows], dv_down)
    dk_high = dk_window[1, span_rows:] + dk_up
    dv_high = dv_window[1, span_rows:] + dv_up
    grad_keys = (
        jnp.concatenate([dk_low, dk_high], axis=0)
        .reshape(2 * span_rows, feature_width)
        .astype(jnp.bfloat16)
    )
    grad_values = (
        jnp.concatenate([dv_low, dv_high], axis=0)
        .reshape(2 * span_rows, feature_width)
        .astype(jnp.bfloat16)
    )
    grad_queries = (
        jnp.concatenate(dq_parts, axis=1).reshape(2 * span_rows, feature_width).astype(jnp.bfloat16)
    )
    return (output, grad_queries, grad_keys, grad_values, grad_weight)


def solution(mesh):
    return jax.shard_map(
        on_device,
        mesh=mesh,
        in_specs=(
            P("tm", "head"),
            P("tm", "head"),
            P("tm", "head"),
            P("head", None),
            P("tm", None),
            P("tm", None),
        ),
        out_specs=(
            P("tm", "head"),
            P("tm", "head"),
            P("tm", "head"),
            P("tm", "head"),
            P("head", "tm"),
        ),
        check_vma=False,
    )
```

profile of v0, /device:TPU:1, one launch (start us, length us, event | category | flops | bytes accessed | tf_op | source)
XLA Modules:
  0.0 279.0 jit_solution(8281436161239510732)
XLA Ops:
  7.2 1.2 fusion.88
  9.3 1.3 collective-permute-start.3
  11.4 5.3 %collective-permute-start.2 = (bf16[512,4,64]{0,2,1:T(8,128)(2,1)}, bf16[512,4,64]{0,2,1:T(8,128)(2,1)}, u32[]{:S(2)}, u32[]{:S(2)}) collective-permute-start(bf16[512,4,64]{0,2,1:T(8,128)(2,1)} %bitcast.9), channel_id=1, source_target_pairs={{0,4},{4,8},{8,12},{12,16},{16,20},{20,24},{24,28},{28,32},{32,36}... | collective-permute-start | bytes 786440 | tf_op jit(solution)/shard_map/ppermute | solution.py:13
  16.8 1.1 fusion.87
  18.7 1.3 collective-permute-start.1
  20.8 4.7 %collective-permute-start = (bf16[512,4,64]{0,2,1:T(8,128)(2,1)}, bf16[512,4,64]{0,2,1:T(8,128)(2,1)}, u32[]{:S(2)}, u32[]{:S(2)}) collective-permute-start(bf16[512,4,64]{0,2,1:T(8,128)(2,1)} %bitcast), channel_id=1, source_target_pairs={{0,4},{4,8},{8,12},{12,16},{16,20},{20,24},{24,28},{28,32},{32,36}... | collective-permute-start | bytes 786440 | tf_op jit(solution)/shard_map/ppermute | solution.py:13
  26.0 2.2 reshape.286
  28.3 1.3 fusion.86
  29.7 1.2 copy.97
  30.9 1.3 copy.98
  32.8 1.1 broadcast_select_fusion
  35.0 1.3 maximum_bitcast_fusion.2
  36.2 1.3 fusion.7
  37.5 1.4 fusion.2
  39.0 1.3 fusion.6
  40.3 1.4 fusion
  41.7 1.2 broadcast_select_fusion.1
  43.9 1.3 maximum_bitcast_fusion
  45.2 1.6 fusion.44
  46.9 1.6 fusion.50
  49.2 1.9 fusion.91
  51.4 3.7 %fusion.90 = f32[1024,1024]{1,0:T(8,128)} fusion(bf16[1024,256]{0,1:T(8,128)(2,1)S(1)} %bitcast.165, bf16[256,1024]{1,0:T(8,128)(2,1)} %param.17), kind=kOutput, calls=%fused_computation.122 | convolution fusion | flops 536870912 | bytes 5242880 | tf_op jit(solution)/shard_map/dot_general | solution.py:104
  55.2 1.0 copy-done.18
  56.2 1.5 convolution_convert_fusion
  57.7 2.0 reshape.287
  59.7 1.3 copy.66
  61.1 1.5 multiply_reduce_fusion
  63.4 5.4 %multiply_convert_fusion.1 = bf16[2,4,256,768]{2,3,1,0:T(8,128)(2,1)S(1)} fusion(f32[2,4,768,256]{3,2,1,0:T(8,128)} %copy-done.4, f32[2,4,256]{2,1,0:T(4,128)S(1)} %get-tuple-element.84, f32[2,4,256]{2,1,0:T(4,128)S(1)} %bitcast.181, pred[2,256,768]{1,2,0:T(8,128)(4,1)} %copy-done.10, bf16[2,512,4,64]{1,3,2,0:T(8,128)(2,1)} %copy.66, ...), kind=kOutput, calls=%fused_computation.4 | convolution fusion | flops 211156992 | bytes 11157504 | tf_op jit(solution)/shard_map/bqhd,bkhd->bhqk/dot_general | solution.py:134
  68.8 1.1 multiply_bitcast_fusion
  70.3 2.5 multiply_convert_fusion
  72.8 2.2 constant_dynamic-update-slice_fusion.1
  75.0 1.2 slice_bitcast_fusion.5
  76.2 1.3 collective-permute-start.4
  77.5 4.9 %collective-permute-start.5 = (f32[512,4,64]{0,2,1:T(8,128)}, f32[512,4,64]{0,2,1:T(8,128)}, u32[]{:S(2)}, u32[]{:S(2)}) collective-permute-start(f32[512,4,64]{0,2,1:T(8,128)} %get-tuple-element.71), channel_id=1, source_target_pairs={{0,4},{4,8},{8,12},{12,16},{16,20},{20,24},{24,28},{28,32},{32,36}... | collective-permute-start | bytes 1572872 | tf_op jit(solution)/shard_map/ppermute | solution.py:13
  82.4 1.9 fusion.26
  85.3 3.0 %constant_dynamic-update-slice_fusion = (f32[2,1024,4,64]{1,3,2,0:T(8,128)S(1)}, f32[2,768,4,64]{1,3,2,0:T(8,128)}) fusion(f32[2,1024,4,64]{1,3,2,0:T(8,128)S(1)} %scatter-add.16, f32[2,4,768,256]{3,2,1,0:T(8,128)S(1)} %bitcast.163, f32[2,4,256]{2,1,0:T(4,128)S(1)} %bitcast.178, pred[2,256,768]{1,2,0:T(8,128)(4,1)S(1)} %get-tuple-element.83, ...), kind=kOutput, calls=%fused_computation.101 | convolution fusion | flops 208011264 | bytes 11673600 | tf_op jit(solution)/shard_map/bhqk,bqhd->bkhd/dot_general | solution.py:131
  88.3 1.2 slice_bitcast_fusion.1
  89.5 1.3 collective-permute-start.6
  90.8 4.8 %collective-permute-start.7 = (f32[512,4,64]{0,2,1:T(8,128)}, f32[512,4,64]{0,2,1:T(8,128)}, u32[]{:S(2)}, u32[]{:S(2)}) collective-permute-start(f32[512,4,64]{0,2,1:T(8,128)} %get-tuple-element.69), channel_id=1, source_target_pairs={{0,4},{4,8},{8,12},{12,16},{16,20},{20,24},{24,28},{28,32},{32,36}... | collective-permute-start | bytes 1572872 | tf_op jit(solution)/shard_map/ppermute | solution.py:13
  97.1 1.6 copy.91
  98.7 1.5 reshape.285
  100.2 1.9 fusion.62
  102.2 1.0 copy.79
  104.6 1.9 fusion.58
  107.5 87.5 %reduce-scatter.5.cloned.1.call-done = f32[256,32]{0,1:T(8,128)} async-done(((f32[256,1024]{0,1:T(8,128)}), f32[256,32]{0,1:T(8,128)}) %reduce-scatter.5.cloned.1.call-update) | async-done | bytes 32784 | tf_op jit(solution)/shard_map/reduce_scatter | solution.py:113
  195.1 1.4 broadcast_multiply_fusion
  196.4 73.7 %reduce-scatter.3.cloned.1.call-done = f32[1024,256]{1,0:T(8,128)} async-done(((f32[1024,1024]{1,0:T(8,128)}), f32[1024,256]{1,0:T(8,128)}) %reduce-scatter.3.cloned.1.call-update) | async-done | bytes 1048592 | tf_op jit(solution)/shard_map/reduce_scatter | solution.py:105
  270.1 2.1 convert_element_type.52
  (104 shorter events, 13.6 us)
Async XLA Ops:
  7.2 42.0 %copy-start = (bf16[1024,1024]{1,0:T(8,128)(2,1)S(1)}, bf16[1024,1024]{1,0:T(8,128)(2,1)}, u32[]{:S(2)}) copy-start(bf16[1024,1024]{1,0:T(8,128)(2,1)} %param.18) | copy-start | bytes 6291460
  7.2 18.3 %copy-start.25 = (s32[8,5]{1,0:T(8,128)S(1)}, s32[8,5]{1,0:T(8,128)}, u32[]{:S(2)}) copy-start(s32[8,5]{1,0:T(8,128)} %param.19) | copy-start | bytes 484
  7.2 187.9 %reduce-scatter.5.cloned.1.call-start = ((), (), s32[]{:S(2)}) async-start(), calls=%async_computation.3 | async-start | bytes 1081344 | tf_op jit(solution)/shard_map/reduce_scatter | solution.py:113
  9.3 23.5 %collective-permute-start.3 = (bf16[512,4,64]{0,2,1:T(8,128)(2,1)}, bf16[512,4,64]{0,2,1:T(8,128)(2,1)}, u32[]{:S(2)}, u32[]{:S(2)}) collective-permute-start(bf16[512,4,64]{0,2,1:T(8,128)(2,1)} %bitcast.11), channel_id=1, source_target_pairs={{4,0},{8,4},{12,8},{16,12},{20,16},{24,20},{28,24},{32,28},{36,32}... | collective-permute-start | bytes 786440 | tf_op jit(solution)/shard_map/ppermute | solution.py:13
  11.4 23.5 %collective-permute-start.2 = (bf16[512,4,64]{0,2,1:T(8,128)(2,1)}, bf16[512,4,64]{0,2,1:T(8,128)(2,1)}, u32[]{:S(2)}, u32[]{:S(2)}) collective-permute-start(bf16[512,4,64]{0,2,1:T(8,128)(2,1)} %bitcast.9), channel_id=1, source_target_pairs={{0,4},{4,8},{8,12},{12,16},{16,20},{20,24},{24,28},{28,32},{32,36}... | collective-permute-start | bytes 786440 | tf_op jit(solution)/shard_map/ppermute | solution.py:13
  18.7 23.0 %collective-permute-start.1 = (bf16[512,4,64]{0,2,1:T(8,128)(2,1)}, bf16[512,4,64]{0,2,1:T(8,128)(2,1)}, u32[]{:S(2)}, u32[]{:S(2)}) collective-permute-start(bf16[512,4,64]{0,2,1:T(8,128)(2,1)} %bitcast.2), channel_id=1, source_target_pairs={{4,0},{8,4},{12,8},{16,12},{20,16},{24,20},{28,24},{32,28},{36,32}... | collective-permute-start | bytes 786440 | tf_op jit(solution)/shard_map/ppermute | solution.py:13
  20.8 23.1 %collective-permute-start = (bf16[512,4,64]{0,2,1:T(8,128)(2,1)}, bf16[512,4,64]{0,2,1:T(8,128)(2,1)}, u32[]{:S(2)}, u32[]{:S(2)}) collective-permute-start(bf16[512,4,64]{0,2,1:T(8,128)(2,1)} %bitcast), channel_id=1, source_target_pairs={{0,4},{4,8},{8,12},{12,16},{16,20},{20,24},{24,28},{28,32},{32,36}... | collective-permute-start | bytes 786440 | tf_op jit(solution)/shard_map/ppermute | solution.py:13
  30.9 8.0 %copy-start.14 = (bf16[2,256,4,64]{1,3,2,0:T(8,128)(2,1)}, bf16[2,256,4,64]{1,3,2,0:T(8,128)(2,1)S(1)}, u32[]{:S(2)}) copy-start(bf16[2,256,4,64]{1,3,2,0:T(8,128)(2,1)S(1)} %copy.97) | copy-start | bytes 786436
  32.3 5.2 %copy-start.12 = (bf16[2,256,4,64]{1,3,2,0:T(8,128)(2,1)}, bf16[2,256,4,64]{1,3,2,0:T(8,128)(2,1)S(1)}, u32[]{:S(2)}) copy-start(bf16[2,256,4,64]{1,3,2,0:T(8,128)(2,1)S(1)} %copy.98) | copy-start | bytes 786436
  32.8 14.0 %copy-start.10 = (pred[2,256,768]{1,2,0:T(8,128)(4,1)}, pred[2,256,768]{1,2,0:T(8,128)(4,1)S(1)}, u32[]{:S(2)}) copy-start(pred[2,256,768]{1,2,0:T(8,128)(4,1)S(1)} %get-tuple-element.82) | copy-start | bytes 1179652
  34.9 4.0 %copy-start.6 = (bf16[1,1024,4,64]{1,3,2,0:T(8,128)(2,1)}, bf16[1,1024,4,64]{1,3,2,0:T(8,128)(2,1)S(1)}, u32[]{:S(2)}) copy-start(bf16[1,1024,4,64]{1,3,2,0:T(8,128)(2,1)S(1)} %maximum_bitcast_fusion.3) | copy-start | bytes 1572868
  36.2 2.7 copy-start.8
  37.5 7.7 %copy-start.1 = (f32[2,4,768,256]{3,2,1,0:T(8,128)}, f32[2,4,768,256]{3,2,1,0:T(8,128)S(1)}, u32[]{:S(2)}) copy-start(f32[2,4,768,256]{3,2,1,0:T(8,128)S(1)} %get-tuple-element.89) | copy-start | bytes 18874372
  40.3 6.6 %copy-start.4 = (f32[2,4,768,256]{3,2,1,0:T(8,128)}, f32[2,4,768,256]{3,2,1,0:T(8,128)S(1)}, u32[]{:S(2)}) copy-start(f32[2,4,768,256]{3,2,1,0:T(8,128)S(1)} %get-tuple-element.91) | copy-start | bytes 18874372
  40.3 6.6 %copy-start.23 = (f32[2,4,256]{2,1,0:T(4,128)}, f32[2,4,256]{2,1,0:T(4,128)S(1)}, u32[]{:S(2)}) copy-start(f32[2,4,256]{2,1,0:T(4,128)S(1)} %get-tuple-element.90) | copy-start | bytes 24580
  41.7 5.2 %copy-start.24 = (f32[2,4,256]{2,1,0:T(4,128)}, f32[2,4,256]{2,1,0:T(4,128)S(1)}, u32[]{:S(2)}) copy-start(f32[2,4,256]{2,1,0:T(4,128)S(1)} %fusion) | copy-start | bytes 24580
  43.9 3.0 %copy-start.19 = (bf16[1,1024,4,64]{1,3,2,0:T(8,128)(2,1)}, bf16[1,1024,4,64]{1,3,2,0:T(8,128)(2,1)S(1)}, u32[]{:S(2)}) copy-start(bf16[1,1024,4,64]{1,3,2,0:T(8,128)(2,1)S(1)} %maximum_bitcast_fusion.1) | copy-start | bytes 1572868
  45.2 1.7 copy-start.21
  46.8 1.7 copy-start.16
  48.5 0.7 copy-start.17
  51.1 219.0 %reduce-scatter.3.cloned.1.call-start = ((), (), s32[]{:S(2)}) async-start(), calls=%async_computation.2 | async-start | bytes 5242880 | tf_op jit(solution)/shard_map/reduce_scatter | solution.py:105
  55.1 1.0 copy-start.18
  61.1 9.1 %slice-start = ((s8[6291456]{0:T(1024)(128)(4,1)}), s8[4194304]{0:T(1024)(128)(4,1)S(1)}, s32[]{:S(2)}) async-start(s8[6291456]{0:T(1024)(128)(4,1)} %bitcast.162), calls=%async_computation.4 | async-start | bytes 8388608
  63.4 5.4 %copy-start.15 = (bf16[2,256,4,64]{1,3,2,0:T(8,128)(2,1)S(1)}, bf16[2,256,4,64]{1,3,2,0:T(8,128)(2,1)}, u32[]{:S(2)}) copy-start(bf16[2,256,4,64]{1,3,2,0:T(8,128)(2,1)} %copy-done.14) | copy-start | bytes 786436
  63.4 6.8 %slice-start.1 = ((s8[6291456]{0:T(1024)(128)(4,1)}), s8[2097152]{0:T(1024)(128)(4,1)S(1)}, s32[]{:S(2)}) async-start(s8[6291456]{0:T(1024)(128)(4,1)} %bitcast.162), calls=%async_computation.5 | async-start | bytes 4194304
  68.8 1.4 copy-start.5
  68.8 1.4 copy-start.20
  68.8 1.4 copy-start.22
  69.9 12.5 %slice-start.2 = ((s8[6291456]{0:T(1024)(128)(4,1)}), s8[4194304]{0:T(1024)(128)(4,1)S(1)}, s32[]{:S(2)}) async-start(s8[6291456]{0:T(1024)(128)(4,1)} %bitcast.166), calls=%async_computation.6 | async-start | bytes 8388608
  70.2 2.5 copy-start.13
  70.2 12.2 %slice-start.3 = ((s8[6291456]{0:T(1024)(128)(4,1)}), s8[2097152]{0:T(1024)(128)(4,1)S(1)}, s32[]{:S(2)}) async-start(s8[6291456]{0:T(1024)(128)(4,1)} %bitcast.166), calls=%async_computation.7 | async-start | bytes 4194304
  72.8 9.7 %copy-start.11 = (pred[2,256,768]{1,2,0:T(8,128)(4,1)S(1)}, pred[2,256,768]{1,2,0:T(8,128)(4,1)}, u32[]{:S(2)}) copy-start(pred[2,256,768]{1,2,0:T(8,128)(4,1)} %copy-done.10) | copy-start | bytes 1179652
  75.0 9.4 %copy-start.2 = (f32[2,1024,4,64]{1,3,2,0:T(8,128)}, f32[2,1024,4,64]{1,3,2,0:T(8,128)S(1)}, u32[]{:S(2)}) copy-start(f32[2,1024,4,64]{1,3,2,0:T(8,128)S(1)} %get-tuple-element.92) | copy-start | bytes 6291460
  76.2 24.0 %collective-permute-start.4 = (f32[512,4,64]{0,2,1:T(8,128)}, f32[512,4,64]{0,2,1:T(8,128)}, u32[]{:S(2)}, u32[]{:S(2)}) collective-permute-start(f32[512,4,64]{0,2,1:T(8,128)} %get-tuple-element.70), channel_id=1, source_target_pairs={{4,0},{8,4},{12,8},{16,12},{20,16},{24,20},{28,24},{32,28},{36,32}... | collective-permute-start | bytes 1572872 | tf_op jit(solution)/shard_map/ppermute | solution.py:13
  77.5 7.2 %copy-start.7 = (bf16[1,1024,4,64]{1,3,2,0:T(8,128)(2,1)S(1)}, bf16[1,1024,4,64]{1,3,2,0:T(8,128)(2,1)}, u32[]{:S(2)}) copy-start(bf16[1,1024,4,64]{1,3,2,0:T(8,128)(2,1)} %copy-done.6) | copy-start | bytes 1572868
  77.5 7.2 %copy-start.9 = (bf16[1,1024,4,64]{1,3,2,0:T(8,128)(2,1)S(1)}, bf16[1,1024,4,64]{1,3,2,0:T(8,128)(2,1)}, u32[]{:S(2)}) copy-start(bf16[1,1024,4,64]{1,3,2,0:T(8,128)(2,1)} %copy-done.8) | copy-start | bytes 1572868
  77.5 22.7 %collective-permute-start.5 = (f32[512,4,64]{0,2,1:T(8,128)}, f32[512,4,64]{0,2,1:T(8,128)}, u32[]{:S(2)}, u32[]{:S(2)}) collective-permute-start(f32[512,4,64]{0,2,1:T(8,128)} %get-tuple-element.71), channel_id=1, source_target_pairs={{0,4},{4,8},{8,12},{12,16},{16,20},{20,24},{24,28},{28,32},{32,36}... | collective-permute-start | bytes 1572872 | tf_op jit(solution)/shard_map/ppermute | solution.py:13
  88.3 7.9 %copy-start.3 = (f32[2,1024,4,64]{1,3,2,0:T(8,128)}, f32[2,1024,4,64]{1,3,2,0:T(8,128)S(1)}, u32[]{:S(2)}) copy-start(f32[2,1024,4,64]{1,3,2,0:T(8,128)S(1)} %get-tuple-element.94) | copy-start | bytes 6291460
  89.5 14.2 %collective-permute-start.6 = (f32[512,4,64]{0,2,1:T(8,128)}, f32[512,4,64]{0,2,1:T(8,128)}, u32[]{:S(2)}, u32[]{:S(2)}) collective-permute-start(f32[512,4,64]{0,2,1:T(8,128)} %get-tuple-element.68), channel_id=1, source_target_pairs={{4,0},{8,4},{12,8},{16,12},{20,16},{24,20},{28,24},{32,28},{36,32}... | collective-permute-start | bytes 1572872 | tf_op jit(solution)/shard_map/ppermute | solution.py:13
  90.8 13.8 %collective-permute-start.7 = (f32[512,4,64]{0,2,1:T(8,128)}, f32[512,4,64]{0,2,1:T(8,128)}, u32[]{:S(2)}, u32[]{:S(2)}) collective-permute-start(f32[512,4,64]{0,2,1:T(8,128)} %get-tuple-element.69), channel_id=1, source_target_pairs={{0,4},{4,8},{8,12},{12,16},{16,20},{20,24},{24,28},{28,32},{32,36}... | collective-permute-start | bytes 1572872 | tf_op jit(solution)/shard_map/ppermute | solution.py:13
Sparse Core Ops, SparseCore 0:
  51.3 143.7 reduce-scatter.4
  197.9 72.1 reduce-scatter.2
where the time goes:
time: 280 us; the launch traced here: 279 us
  waiting for transfers between devices  163 us (58%)
  matrix products  30.4 us (11%)
  local copies, waits for them, and re-layouts  25.2 us (9%)
  starting transfers between devices  25.2 us (9%)
  other arithmetic  20.8 us (7%)
  between operations  14.7 us (5%)
    reduce_scatter x1, waiting for transfers between devices, on_device(): lax.psum_scatter(weight_term, 'tm', scatter_dimension=1, tiled=True)  87.5 us
    reduce_scatter x1, waiting for transfers between devices, on_device(): lax.psum_scatter(partial_value, 'head', scatter_dimension=1, tiled=True)  73.7 us
    ppermute x8, starting transfers between devices, from_behind(): return lax.ppermute(x, axis, pairs)  24.9 us
    unnamed x67, local copies, waits for them, and re-layouts  8.89 us
    dot_general x2, matrix products, on_device(): jnp.einsum('bqhd,bkhd->bhqk', g_group, v_group, preferred_element_type=jn...  7.89 us
  transfers between devices with their start and end apart: 10, of which 4 were waited for; matrix products, arithmetic and copies ran while one was open for 23% of the time, Pallas kernels for 0%

commit v1 on v0

v1 whole, which is shorter than its diff:
```python
import jax
import jax.numpy as jnp
from jax import lax
from jax.experimental import pallas as pl
from jax.experimental.pallas import tpu as pltpu
from jax.sharding import PartitionSpec as P

HD = 64
T = 128
F32 = jnp.float32
BF16 = jnp.bfloat16


def ring(x, by):
    n = lax.axis_size("tm")
    return lax.ppermute(x, "tm", [(i, (i + by) % n) for i in range(n)])


def core_swap(x):
    return lax.ppermute(x, "head", [(0, 1), (1, 0), (2, 3), (3, 2)])


def chip_swap(x):
    return lax.ppermute(x, "head", [(0, 2), (2, 0), (1, 3), (3, 1)])


def nt(a, b):
    return lax.dot_general(a, b, (((1,), (1,)), ((), ())), preferred_element_type=F32)


def nn(a, b):
    return jnp.dot(a, b, preferred_element_type=F32)


def head_stack(x, heads):
    owner = lax.broadcasted_iota(jnp.int32, x.shape, 1) // HD
    zero = jnp.zeros_like(x)
    return jnp.concatenate([jnp.where(owner == h, x, zero) for h in range(heads)], axis=0)


def own_blocks(x, heads):
    parts = []
    for p in range(heads // 2):
        parts += [x[p][:HD, :T], x[p][HD:, T:]]
    return parts


def forward_kernel(where, lists, q, k, v, kvu, kvd, ga, att_o, p_o, g_o, del_o, kw, vt):
    width = q.shape[1]
    heads = width // HD
    span = k.shape[0] // 2
    n_tile = span // T
    reach = n_tile + 1
    last_tm = where[1] - 1
    is_last = where[0] == last_tm
    for half in range(2):
        if half == 0:
            kp, vp = kvu[:, :width], kvu[:, width:]
        else:
            kp = jnp.where(is_last, k[:span], kvd[:, :width])
            vp = jnp.where(is_last, v[:span], kvd[:, width:])
        own = pl.ds(half * span, span)
        kw[half, :span] = kp
        kw[half, span:] = k[own]
        vt[half, :, :span] = vp.T
        vt[half, :, span:] = v[own].T
    for half in range(2):
        piece = where[0] if half == 0 else 2 * where[1] - 1 - where[0]
        for j in range(n_tile):
            row = half * n_tile + j
            rows = pl.ds(row * T, T)
            win = pl.ds(j * T, reach * T)
            qm = head_stack(q[rows] * BF16(HD**-0.5), heads)
            s = nt(kw[half, win], qm)
            tiles = []
            for w in range(reach):
                t = piece * n_tile + j - n_tile + w
                hit = lists[row, 0] == t
                for c in range(1, lists.shape[1]):
                    hit = hit | (lists[row, c] == t)
                hit = hit & (t >= 0)
                sw = s[w * T : (w + 1) * T]
                ok = jnp.where(hit, 1, 0)
                if w == reach - 1:
                    key = lax.broadcasted_iota(jnp.int32, sw.shape, 0)
                    qry = lax.broadcasted_iota(jnp.int32, sw.shape, 1) % T
                    sw = jnp.where(jnp.where(key <= qry, ok, 0) > 0, sw, -1e30)
                else:
                    sw = jnp.where(ok > 0, sw, -1e30)
                tiles.append(sw)
            s = jnp.concatenate(tiles, axis=0)
            m = jnp.max(s, axis=0, keepdims=True)
            p = jnp.exp(s - m)
            inv = 1.0 / jnp.sum(p, axis=0, keepdims=True)
            pb = p.astype(BF16)
            p_o[row] = pb
            o2 = [
                nn(vt[half, 2 * HD * i : 2 * HD * (i + 1), win], pb[:, 2 * T * i : 2 * T * (i + 1)])
                for i in range(heads // 2)
            ]
            o = own_blocks(o2, heads)
            at, gt, dl = [], [], []
            for h in range(heads):
                iv = inv[:, h * T : (h + 1) * T]
                a = (o[h] * iv).astype(BF16)
                g = (ga[h * HD : (h + 1) * HD, rows] * iv).astype(BF16)
                at.append(a)
                gt.append(g)
                dl.append(jnp.sum(a.astype(F32) * g.astype(F32), axis=0, keepdims=True))
            att_o[rows] = jnp.concatenate(at, axis=0).T
            g_o[rows] = jnp.concatenate(gt, axis=0).T
            del_o[row] = jnp.concatenate(dl, axis=1)


def back_prev_kernel(where, q, k, v, kvu, kvd, p, g, dl, ret_o, dq_o, kt, acc):
    width = q.shape[1]
    heads = width // HD
    span = k.shape[0] // 2
    n_tile = span // T
    is_last = where[0] == where[1] - 1
    for half in range(2):
        if half == 0:
            kp, vp = kvu[:, :width], kvu[:, width:]
        else:
            kp = jnp.where(is_last, k[:span], kvd[:, :width])
            vp = jnp.where(is_last, v[:span], kvd[:, width:])
        kt[...] = kp.T
        for j in range(n_tile):
            row = half * n_tile + j
            rows = pl.ds(row * T, T)
            size = span - j * T
            gm = head_stack(g[rows], heads)
            qm = head_stack(q[rows] * BF16(HD**-0.5), heads)
            pb = p[row, :size]
            dp = nt(vp[j * T :], gm)
            ds = (pb.astype(F32) * (dp - dl[row])).astype(BF16)
            d2 = [
                nn(kt[2 * HD * i : 2 * HD * (i + 1), j * T :], ds[:, 2 * T * i : 2 * T * (i + 1)])
                for i in range(heads // 2)
            ]
            dq_o[:, rows] = jnp.concatenate(own_blocks(d2, heads), axis=0)
            dk, dv = nn(ds, qm), nn(pb, gm)
            if j == 0:
                acc[:, :width] = dk
                acc[:, width:] = dv
            else:
                acc[j * T :, :width] += dk
                acc[j * T :, width:] += dv
        ret_o[half] = acc[...].astype(BF16)


def back_own_kernel(q, k, v, p, g, dl, dqp, dq_o, dk_o, dv_o, kt):
    width = q.shape[1]
    heads = width // HD
    span = k.shape[0] // 2
    n_tile = span // T
    for half in range(2):
        own = half * span
        kt[...] = k[own : own + span].T
        for j in reversed(range(n_tile)):
            row = half * n_tile + j
            rows = pl.ds(row * T, T)
            size = (j + 1) * T
            gm = head_stack(g[rows], heads)
            qm = head_stack(q[rows] * BF16(HD**-0.5), heads)
            pb = p[row, span - j * T :]
            dp = nt(v[own : own + size], gm)
            ds = (pb.astype(F32) * (dp - dl[row])).astype(BF16)
            d2 = [
                nn(kt[2 * HD * i : 2 * HD * (i + 1), :size], ds[:, 2 * T * i : 2 * T * (i + 1)])
                for i in range(heads // 2)
            ]
            dq = jnp.concatenate(own_blocks(d2, heads), axis=0) + dqp[:, rows]
            dq_o[rows] = (dq * HD**-0.5).astype(BF16).T
            dk, dv = nn(ds, qm), nn(pb, gm)
            if j == n_tile - 1:
                dk_o[own : own + size] = dk
                dv_o[own : own + size] = dv
            else:
                dk_o[own : own + size] += dk
                dv_o[own : own + size] += dv


def call(body, outs, scratch, scalars, flops, *args):
    vm = pl.BlockSpec(memory_space=pltpu.VMEM)
    sm = pl.BlockSpec(memory_space=pltpu.SMEM)
    return pl.pallas_call(
        body,
        out_shape=outs,
        in_specs=[sm] * scalars + [vm] * (len(args) - scalars),
        out_specs=[vm] * len(outs),
        scratch_shapes=scratch,
        compiler_params=pltpu.CompilerParams(vmem_limit_bytes=56 << 20),
        cost_estimate=pl.CostEstimate(flops=flops, transcendentals=0, bytes_accessed=8 << 20),
    )(*args)


def on_device(queries, keys, values, out_weight, grad_output, tile_lists):
    rows, width = queries.shape
    heads = width // HD
    span = rows // 2
    n_tile = span // T
    n_row = 2 * n_tile
    tm_count = lax.axis_size("tm")
    tm_index = lax.axis_index("tm")
    head_index = lax.axis_index("head")
    shape = jax.ShapeDtypeStruct
    is_last = tm_index == tm_count - 1
    where = jnp.stack([tm_index, jnp.int32(tm_count)]).astype(jnp.int32)

    kv = jnp.concatenate([keys, values], axis=1)
    kvu = ring(kv[:span], 1)
    kvd = ring(kv[span:], -1)

    w4 = out_weight.reshape(width, 2, 2, width)
    core = head_index % 2
    chip = head_index // 2
    w_core = lax.dynamic_index_in_dim(w4, core, axis=2, keepdims=False)
    w_send = lax.dynamic_index_in_dim(w4, 1 - core, axis=2, keepdims=False)
    w_recv = core_swap(w_send.reshape(width, 2 * width)).reshape(width, 2, width)

    ga = lax.dot_general(out_weight, grad_output, (((1,), (1,)), ((), ())), preferred_element_type=F32)

    att, p, g, dl = call(
        forward_kernel,
        [
            shape((rows, width), BF16),
            shape((n_row, (n_tile + 1) * T, heads * T), BF16),
            shape((rows, width), BF16),
            shape((n_row, 1, heads * T), F32),
        ],
        [pltpu.VMEM((2, 2 * span, width), BF16), pltpu.VMEM((2, width, 2 * span), BF16)],
        2,
        4 * 10**9,
        where,
        tile_lists,
        queries,
        keys,
        values,
        kvu,
        kvd,
        ga,
    )

    att_other = core_swap(att)
    wt = lax.dot_general(grad_output, att, (((0,), (0,)), ((), ())), preferred_element_type=F32)
    there = lax.dynamic_index_in_dim(w_core, 1 - chip, axis=1, keepdims=False)
    there_o = lax.dynamic_index_in_dim(w_recv, 1 - chip, axis=1, keepdims=False)
    here = lax.dynamic_index_in_dim(w_core, chip, axis=1, keepdims=False)
    here_o = lax.dynamic_index_in_dim(w_recv, chip, axis=1, keepdims=False)
    out_recv = chip_swap((nn(att, there) + nn(att_other, there_o)).astype(BF16))

    ret, dqp = call(
        back_prev_kernel,
        [shape((2, span, 2 * width), BF16), shape((width, rows), F32)],
        [pltpu.VMEM((width, span), BF16), pltpu.VMEM((span, 2 * width), F32)],
        1,
        4 * 10**9,
        where,
        queries,
        keys,
        values,
        kvu,
        kvd,
        p,
        g,
        dl,
    )
    back_low = ring(ret[0], -1)
    back_high = ring(ret[1], 1)

    w_split = wt.astype(BF16).reshape(tm_count, -1, width)
    w_parts = lax.all_to_all(w_split, "tm", 0, 0, tiled=True)

    dq, dk, dv = call(
        back_own_kernel,
        [shape((rows, width), BF16), shape((rows, width), F32), shape((rows, width), F32)],
        [pltpu.VMEM((width, span), BF16)],
        0,
        4 * 10**9,
        queries,
        keys,
        values,
        p,
        g,
        dl,
        dqp,
    )
    output = (nn(att, here) + nn(att_other, here_o) + out_recv.astype(F32)).astype(BF16)
    low = jnp.where(is_last, ret[1], back_low).astype(F32)
    high = jnp.where(tm_index == 0, jnp.zeros_like(back_high), back_high).astype(F32)
    halo = jnp.concatenate([low, high], axis=0)
    grad_keys = (dk + halo[:, :width]).astype(BF16)
    grad_values = (dv + halo[:, width:]).astype(BF16)
    scale = (tm_count * rows) ** -0.5
    grad_weight = (jnp.sum(w_parts.astype(F32), axis=0) * scale).T
    return output, dq, grad_keys, grad_values, grad_weight


def solution(mesh):
    return jax.shard_map(
        on_device,
        mesh=mesh,
        in_specs=(
            P("tm", "head"),
            P("tm", "head"),
            P("tm", "head"),
            P("head", None),
            P("tm", None),
            P("tm", None),
        ),
        out_specs=(
            P("tm", "head"),
            P("tm", "head"),
            P("tm", "head"),
            P("tm", "head"),
            P("head", "tm"),
        ),
        check_vma=False,
    )
```

time: 280 us -> 102 us (0.36)
  waiting for transfers between devices: 163 us -> 28.3 us
  Pallas kernels: 0 us -> 27.6 us
  matrix products: 30.4 us -> 8.61 us
  local copies, waits for them, and re-layouts: 25.2 us -> 7.38 us
  other arithmetic: 20.8 us -> 5 us
  between operations: 14.7 us -> 0.77 us
    reduce_scatter x2 -> x0, waiting for transfers between devices: 161 us -> none  [the longest x1 87.5 us: on_device(): lax.psum_scatter(weight_term, 'tm', scatter_dimension=1, tiled=True)]
    pallas_call x0 -> x3, Pallas kernels: none -> 27.6 us  [call(): pl.pallas_call(body, out_shape=outs, in_specs=[sm] * scalars + [vm] * (le...]
    ppermute x8 -> x7, waiting for transfers between devices: 1.43 us -> 28.3 us  [the longest x4 21.6 us: ring(): return lax.ppermute(x, 'tm', [(i, (i + by) % n) for i in range(n)])]
    dot_general x15 -> x6, matrix products: 30.4 us -> 8.61 us  [the longest x4 4.21 us: nn(): return jnp.dot(a, b, preferred_element_type=F32)]
    another operation x6 -> x1, other arithmetic: 8.31 us -> 0.64 us  [on_device(): where = jnp.stack([tm_index, jnp.int32(tm_count)]).astype(jnp.int32)]
    unnamed x67 -> x16, local copies, waits for them, and re-layouts: 8.89 us -> 1.47 us
    ppermute x8 -> x7, starting transfers between devices: 24.9 us -> 18.6 us  [the longest x4 13.3 us: ring(): return lax.ppermute(x, 'tm', [(i, (i + by) % n) for i in range(n)])]
    slice x8 -> x1, local copies, waits for them, and re-layouts: 7.02 us -> 1.03 us  [on_device(): kvd = ring(kv[span:], -1)]
  transfers between devices with their start and end apart: 10 -> 8, of which waited for: 4 -> 5; matrix products, arithmetic and copies ran while one was open for 23% -> 16% of each run, Pallas kernels for 0% -> 27%
where the time goes in v1:
time: 102 us; the launch traced here: 101 us
  waiting for transfers between devices  28.3 us (28%)
  Pallas kernels  27.6 us (27%)
  starting transfers between devices  23.4 us (23%)
  matrix products  8.61 us (8%)
  local copies, waits for them, and re-layouts  7.38 us (7%)
  other arithmetic  5 us (5%)
    pallas_call x3, Pallas kernels, call(): pl.pallas_call(body, out_shape=outs, in_specs=[sm] * scalars + [vm] * (le...  27.6 us
    ppermute x4, waiting for transfers between devices, ring(): return lax.ppermute(x, 'tm', [(i, (i + by) % n) for i in range(n)])  21.6 us
    ppermute x4, starting transfers between devices, ring(): return lax.ppermute(x, 'tm', [(i, (i + by) % n) for i in range(n)])  13.3 us
    ppermute x1, waiting for transfers between devices, chip_swap(): return lax.ppermute(x, 'head', [(0, 2), (2, 0), (1, 3), (3, 1)])  6.66 us
    all_to_all x1, starting transfers between devices, on_device(): w_parts = lax.all_to_all(w_split, 'tm', 0, 0, tiled=True)  4.8 us
    dot_general x4, matrix products, nn(): return jnp.dot(a, b, preferred_element_type=F32)  4.21 us
    ppermute x2, starting transfers between devices, core_swap(): return lax.ppermute(x, 'head', [(0, 1), (1, 0), (2, 3), (3, 2)])  2.82 us
    dot_general x1, matrix products, on_device(): lax.dot_general(grad_output, att, (((0,), (0,)), ((), ())), preferred_ele...  2.65 us
  transfers between devices with their start and end apart: 8, of which 5 were waited for; matrix products, arithmetic and copies ran while one was open for 16% of the time, Pallas kernels for 27%

profile of v1, /device:TPU:1, one launch (start us, length us, event | category | flops | bytes accessed | tf_op | source)
XLA Modules:
  0.0 101.1 jit_solution(6156264610954367599)
XLA Ops:
  0.6 0.0 copy-start
  0.6 0.0 copy-start.4
  0.7 1.2 %constant_dynamic-update-slice_fusion.1 = bf16[1024,512]{1,0:T(8,128)(2,1)S(1)} fusion(bf16[1024,256]{1,0:T(8,128)(2,1)} %k.5), kind=kLoop, calls=%fused_computation.29 | loop fusion | bytes 1048576
  1.9 1.1 %constant_dynamic-update-slice_fusion = bf16[1024,512]{1,0:T(8,128)(2,1)S(1)} fusion(bf16[1024,512]{1,0:T(8,128)(2,1)S(1)} %constant_dynamic-update-slice_fusion.1, bf16[1024,256]{1,0:T(8,128)(2,1)} %v.5), kind=kLoop, calls=%fused_computation.28 | loop fusion | bytes 1048576 | tf_op jit(solution)/shard_map/concatenate | solution.py:211
  3.0 1.0 %fusion.20 = (bf16[512,512]{1,0:T(8,128)(2,1)}, bf16[512,512]{1,0:T(8,128)(2,1)}) fusion(bf16[1024,512]{1,0:T(8,128)(2,1)S(1)} %constant_dynamic-update-slice_fusion), kind=kLoop, calls=%fused_computation.36 | loop fusion | bytes 2097152 | tf_op jit(solution)/shard_map/slice | solution.py:213
  4.0 8.0 %collective-permute-start.1 = (bf16[512,512]{1,0:T(8,128)(2,1)}, bf16[512,512]{1,0:T(8,128)(2,1)}, u32[]{:S(2)}, u32[]{:S(2)}) collective-permute-start(bf16[512,512]{1,0:T(8,128)(2,1)} %get-tuple-element.27), channel_id=1, source_target_pairs={{0,124},{4,0},{8,4},{12,8},{16,12},{20,16},{24,20},{28,24},{32,28}... | collective-permute-start | bytes 1572872 | tf_op jit(solution)/shard_map/ppermute | solution.py:16
  12.0 0.0 collective-permute-start
  12.0 0.0 copy-done.4
  12.0 0.2 copy.15
  12.2 0.7 constant_dynamic-slice_fusion
  12.9 1.0 collective-permute-start.3
  13.9 0.6 pad_add_fusion.where
  14.5 0.0 copy-done
  14.5 1.8 %fusion.21.ga = f32[256,1024]{1,0:T(8,128)} fusion(bf16[256,1024]{1,0:T(8,128)(2,1)S(1)} %copy-done.4, bf16[1024,1024]{1,0:T(8,128)(2,1)S(1)} %copy-done), kind=kOutput, calls=%fused_computation.37 | convolution fusion | flops 536870912 | bytes 3670016 | tf_op jit(solution)/shard_map/dot_general | solution.py:222
  16.3 6.6 %collective-permute-done.1.kvd = bf16[512,512]{1,0:T(8,128)(2,1)} collective-permute-done((bf16[512,512]{1,0:T(8,128)(2,1)}, bf16[512,512]{1,0:T(8,128)(2,1)}, u32[]{:S(2)}, u32[]{:S(2)}) %collective-permute-start.1) | collective-permute-done | bytes 524320 | tf_op jit(solution)/shard_map/ppermute | solution.py:16
  22.9 6.1 %collective-permute-done.kvu = bf16[512,512]{1,0:T(8,128)(2,1)} collective-permute-done((bf16[512,512]{1,0:T(8,128)(2,1)}, bf16[512,512]{1,0:T(8,128)(2,1)}, u32[]{:S(2)}, u32[]{:S(2)}) %collective-permute-start) | collective-permute-done | bytes 524320 | tf_op jit(solution)/shard_map/ppermute | solution.py:16
  29.0 10.5 %shard_map.101 = (bf16[1024,256]{1,0:T(8,128)(2,1)}, bf16[8,640,512]{2,1,0:T(8,128)(2,1)}, bf16[1024,256]{1,0:T(8,128)(2,1)}, f32[8,1,512]{2,1,0:T(1,128)}) custom-call(s32[2]{0:T(128)} %pad_add_fusion.where, s32[8,5]{1,0:T(8,128)} %lists.1, bf16[1024,256]{1,0:T(8,128)(2,1)} %q.5, bf16[1024,256]{1,0:T(8,128)(2,1)} %k.5, bf16[1024,256]{1,0:T(8,128)(2,1)} %v.5, ...), custom_call_target="tpu_custom_call" | custom-call | flops 4000000000 | bytes 8388608 | tf_op jit(solution)/shard_map/pallas_call | solution.py:187
  39.5 2.6 %fusion.3 = bf16[1024,256]{0,1:T(8,128)(2,1)} fusion(bf16[1024,256]{1,0:T(8,128)(2,1)} %get-tuple-element.14, bf16[1024,1024]{1,0:T(8,128)(2,1)S(1)} %copy-done), kind=kOutput, calls=%fused_computation.6 | convolution fusion | flops 537133056 | bytes 3145728 | tf_op jit(solution)/shard_map/dot_general | solution.py:246
  42.2 0.0 copy-done.1
  42.2 1.9 %collective-permute-start.2 = (bf16[1024,256]{1,0:T(8,128)(2,1)S(1)}, bf16[1024,256]{1,0:T(8,128)(2,1)}, u32[]{:S(2)}, u32[]{:S(2)}) collective-permute-start(bf16[1024,256]{1,0:T(8,128)(2,1)S(1)} %copy-done.1), channel_id=1, source_target_pairs={{0,1},{1,0},{2,3},{3,2},{4,5},{5,4},{6,7},{7,6},{8,9},{9,8},{10,11... | collective-permute-start | bytes 1572872 | tf_op jit(solution)/shard_map/ppermute | solution.py:20
  44.1 2.0 %copy.20 = bf16[1024,256]{1,0:T(8,128)(2,1)} copy(bf16[1024,256]{0,1:T(8,128)(2,1)} %fusion.3) | data formatting | bytes 1048576 | tf_op jit(solution)/shard_map/convert_element_type | solution.py:272
  46.1 4.8 %all-to-all-start = ((bf16[32,32,256]{2,1,0:T(8,128)(2,1)}), bf16[32,32,256]{2,1,0:T(8,128)(2,1)}, u32[]{:S(2)}, u32[]{:S(2)}) async-start(bf16[32,32,256]{2,1,0:T(8,128)(2,1)} %bitcast.42), calls=%async_computation | async-start | bytes 1048576 | tf_op jit(solution)/shard_map/all_to_all | solution.py:273
  50.9 8.4 %shard_map.102 = (bf16[2,512,512]{2,1,0:T(8,128)(2,1)}, f32[256,1024]{1,0:T(8,128)}) custom-call(s32[2]{0:T(128)} %pad_add_fusion.where, bf16[1024,256]{1,0:T(8,128)(2,1)} %q.5, bf16[1024,256]{1,0:T(8,128)(2,1)} %k.5, bf16[1024,256]{1,0:T(8,128)(2,1)} %v.5, bf16[512,512]{1,0:T(8,128)(2,1)} %collective-permute-done.kvu, ...), custom_call_target="tpu_custom_call" | custom-call | flops 4000000000 | bytes 8388608 | tf_op jit(solution)/shard_map/pallas_call | solution.py:187
  59.3 8.6 %shard_map.103 = (bf16[1024,256]{1,0:T(8,128)(2,1)}, f32[1024,256]{1,0:T(8,128)}, f32[1024,256]{1,0:T(8,128)}) custom-call(bf16[1024,256]{1,0:T(8,128)(2,1)} %q.5, bf16[1024,256]{1,0:T(8,128)(2,1)} %k.5, bf16[1024,256]{1,0:T(8,128)(2,1)} %v.5, bf16[8,640,512]{2,1,0:T(8,128)(2,1)} %get-tuple-element.15.p, bf16[1024,256]{1,0:T(8,128)(2,1)} %get-tuple-element.16.g, ...), custom_call_target="tpu_custom_call" | custom-call | flops 4000000000 | bytes 8388608 | tf_op jit(solution)/shard_map/pallas_call | solution.py:187
  68.0 0.0 copy-done.2
  68.0 1.0 %slice_bitcast_fusion = (bf16[512,512]{1,0:T(8,128)(2,1)}, bf16[512,512]{1,0:T(8,128)(2,1)}) fusion(bf16[2,512,512]{2,1,0:T(8,128)(2,1)S(1)} %copy-done.2), kind=kLoop, calls=%fused_computation.13 | loop fusion | bytes 2097152 | tf_op jit(solution)/shard_map/squeeze | solution.py:269
  69.0 5.3 %collective-permute-start.5 = (bf16[512,512]{1,0:T(8,128)(2,1)}, bf16[512,512]{1,0:T(8,128)(2,1)}, u32[]{:S(2)}, u32[]{:S(2)}) collective-permute-start(bf16[512,512]{1,0:T(8,128)(2,1)} %get-tuple-element.25), channel_id=1, source_target_pairs={{0,124},{4,0},{8,4},{12,8},{16,12},{20,16},{24,20},{28,24},{32,28}... | collective-permute-start | bytes 1572872 | tf_op jit(solution)/shard_map/ppermute | solution.py:16
  74.3 0.0 collective-permute-start.6
  74.3 0.0 all-to-all-done
  74.3 1.1 %convert_reduce_fusion = f32[32,256]{1,0:T(8,128)S(1)} fusion(bf16[32,32,256]{2,1,0:T(8,128)(2,1)} %all-to-all-done), kind=kLoop, calls=%fused_computation.12 | loop fusion | flops 516096 | bytes 557056 | tf_op jit(solution)/shard_map/reduce_sum | solution.py:296
  75.4 0.6 multiply_bitcast_fusion
  76.0 0.0 collective-permute-done.3
  76.0 0.0 collective-permute-done.2
  76.0 1.4 %fusion.6 = f32[1024,256]{1,0:T(8,128)S(1)} fusion(bf16[1024,256]{1,0:T(8,128)(2,1)} %collective-permute-done.2, bf16[256,2,256]{0,2,1:T(8,128)(2,1)S(1)} %bitcast.43, s32[]{:T(128)S(6)} %select_n.54), kind=kOutput, calls=%fused_computation.17 | convolution fusion | flops 134217728 | bytes 1703940 | tf_op jit(solution)/shard_map/dot_general | solution.py:32
  77.4 0.0 copy-start.3
  77.4 0.3 fusion.2
  77.8 2.5 %collective-permute-start.4 = (bf16[1024,256]{1,0:T(8,128)(2,1)S(1)}, bf16[1024,256]{1,0:T(8,128)(2,1)S(1)}, u32[]{:S(2)}, u32[]{:S(2)}) collective-permute-start(bf16[1024,256]{1,0:T(8,128)(2,1)S(1)} %fusion.2), channel_id=1, source_target_pairs={{0,2},{2,0},{1,3},{3,1},{4,6},{6,4},{5,7},{7,5},{8,10},{10,8},{9,1... | collective-permute-start | bytes 1572872 | tf_op jit(solution)/shard_map/ppermute | solution.py:24
  80.3 1.4 %fusion.9 = f32[1024,256]{1,0:T(8,128)S(1)} fusion(bf16[1024,256]{1,0:T(8,128)(2,1)} %collective-permute-done.2, bf16[256,2,256]{0,2,1:T(8,128)(2,1)S(1)} %bitcast.44, s32[]{:T(128)S(6)} %select_n.48), kind=kOutput, calls=%fused_computation.20 | convolution fusion | flops 134217728 | bytes 1703940 | tf_op jit(solution)/shard_map/dot_general | solution.py:32
  81.7 4.0 %collective-permute-done.5 = bf16[512,512]{1,0:T(8,128)(2,1)} collective-permute-done((bf16[512,512]{1,0:T(8,128)(2,1)}, bf16[512,512]{1,0:T(8,128)(2,1)}, u32[]{:S(2)}, u32[]{:S(2)}) %collective-permute-start.5) | collective-permute-done | bytes 524320 | tf_op jit(solution)/shard_map/ppermute | solution.py:16
  85.6 0.0 copy-done.3
  85.6 1.1 %broadcast_select_fusion.1 = bf16[512,512]{1,0:T(8,128)(2,1)S(1)} fusion(bf16[512,512]{1,0:T(8,128)(2,1)} %collective-permute-done.5, pred[]{:T(512)S(6)} %eq.8, bf16[2,512,512]{2,1,0:T(8,128)(2,1)S(1)} %copy-done.3), kind=kLoop, calls=%fused_computation.16 | loop fusion | flops 262144 | bytes 1572865 | tf_op jit(solution)/shard_map/jit(_where)/select_n | solution.py:290
  86.7 0.0 copy-start.5
  86.7 0.0 copy-start.6
  86.7 5.0 %collective-permute-done.6 = bf16[512,512]{1,0:T(8,128)(2,1)} collective-permute-done((bf16[512,512]{1,0:T(8,128)(2,1)}, bf16[512,512]{1,0:T(8,128)(2,1)}, u32[]{:S(2)}, u32[]{:S(2)}) %collective-permute-start.6) | collective-permute-done | bytes 524320 | tf_op jit(solution)/shard_map/ppermute | solution.py:16
  91.8 0.3 maximum_convert_fusion
  92.1 1.2 %fusion.4 = (bf16[1024,256]{1,0:T(8,128)(2,1)}, bf16[1024,256]{1,0:T(8,128)(2,1)}) fusion(f32[1024,256]{1,0:T(8,128)S(1)} %copy-done.6, f32[1024,512]{1,0:T(8,128)S(1)} %maximum_convert_fusion, f32[1024,256]{1,0:T(8,128)S(1)} %copy-done.5), kind=kLoop, calls=%fused_computation.8 | loop fusion | flops 1048576 | bytes 5242880 | tf_op jit(solution)/shard_map/convert_element_type | solution.py:294
  93.3 6.7 %collective-permute-done.4 = bf16[1024,256]{1,0:T(8,128)(2,1)S(1)} collective-permute-done((bf16[1024,256]{1,0:T(8,128)(2,1)S(1)}, bf16[1024,256]{1,0:T(8,128)(2,1)S(1)}, u32[]{:S(2)}, u32[]{:S(2)}) %collective-permute-start.4) | collective-permute-done | bytes 524320 | tf_op jit(solution)/shard_map/ppermute | solution.py:24
  99.9 1.1 %fusion.1 = bf16[1024,256]{1,0:T(8,128)(2,1)} fusion(f32[1024,256]{1,0:T(8,128)S(1)} %fusion.9, bf16[1024,256]{1,0:T(8,128)(2,1)S(1)} %copy-done.1, bf16[1024,256]{1,0:T(8,128)(2,1)S(1)} %collective-permute-done.4, bf16[256,2,2,256]{0,3,2,1:T(8,128)(2,1)S(1)} %bitcast.41, s32[]{:T(128)S(6)} %select_n.49, s32[]{:T(128)S(6)} %select_n.52), kind=kOutput, calls=%fused_computation.3 | convolution fusion | flops 135266304 | bytes 2752520 | tf_op jit(solution)/shard_map/dot_general | solution.py:32
  (5 shorter events, 0.0 us)
Async XLA Ops:
  0.6 13.9 %copy-start = (bf16[1024,1024]{1,0:T(8,128)(2,1)S(1)}, bf16[1024,1024]{1,0:T(8,128)(2,1)}, u32[]{:S(2)}) copy-start(bf16[1024,1024]{1,0:T(8,128)(2,1)} %param.10) | copy-start | bytes 6291460
  0.6 11.3 %copy-start.4 = (bf16[256,1024]{1,0:T(8,128)(2,1)S(1)}, bf16[256,1024]{1,0:T(8,128)(2,1)}, u32[]{:S(2)}) copy-start(bf16[256,1024]{1,0:T(8,128)(2,1)} %param.9) | copy-start | bytes 1572868
  4.0 18.9 %collective-permute-start.1 = (bf16[512,512]{1,0:T(8,128)(2,1)}, bf16[512,512]{1,0:T(8,128)(2,1)}, u32[]{:S(2)}, u32[]{:S(2)}) collective-permute-start(bf16[512,512]{1,0:T(8,128)(2,1)} %get-tuple-element.27), channel_id=1, source_target_pairs={{0,124},{4,0},{8,4},{12,8},{16,12},{20,16},{24,20},{28,24},{32,28}... | collective-permute-start | bytes 1572872 | tf_op jit(solution)/shard_map/ppermute | solution.py:16
  12.0 17.0 %collective-permute-start = (bf16[512,512]{1,0:T(8,128)(2,1)}, bf16[512,512]{1,0:T(8,128)(2,1)}, u32[]{:S(2)}, u32[]{:S(2)}) collective-permute-start(bf16[512,512]{1,0:T(8,128)(2,1)} %get-tuple-element.28), channel_id=1, source_target_pairs={{0,4},{4,8},{8,12},{12,16},{16,20},{20,24},{24,28},{28,32},{32,36}... | collective-permute-start | bytes 1572872 | tf_op jit(solution)/shard_map/ppermute | solution.py:16
  12.9 63.1 %collective-permute-start.3 = (bf16[256,512]{0,1:T(8,128)(2,1)}, bf16[256,512]{0,1:T(8,128)(2,1)S(1)}, u32[]{:S(2)}, u32[]{:S(2)}) collective-permute-start(bf16[256,512]{0,1:T(8,128)(2,1)} %bitcast.3), channel_id=1, source_target_pairs={{0,1},{1,0},{2,3},{3,2},{4,5},{5,4},{6,7},{7,6},{8,9},{9,8},{10,11... | collective-permute-start | bytes 786440 | tf_op jit(solution)/shard_map/ppermute | solution.py:20
  39.5 2.7 %copy-start.1 = (bf16[1024,256]{1,0:T(8,128)(2,1)S(1)}, bf16[1024,256]{1,0:T(8,128)(2,1)}, u32[]{:S(2)}) copy-start(bf16[1024,256]{1,0:T(8,128)(2,1)} %get-tuple-element.14) | copy-start | bytes 1572868
  42.2 33.8 %collective-permute-start.2 = (bf16[1024,256]{1,0:T(8,128)(2,1)S(1)}, bf16[1024,256]{1,0:T(8,128)(2,1)}, u32[]{:S(2)}, u32[]{:S(2)}) collective-permute-start(bf16[1024,256]{1,0:T(8,128)(2,1)S(1)} %copy-done.1), channel_id=1, source_target_pairs={{0,1},{1,0},{2,3},{3,2},{4,5},{5,4},{6,7},{7,6},{8,9},{9,8},{10,11... | collective-permute-start | bytes 1572872 | tf_op jit(solution)/shard_map/ppermute | solution.py:20
  46.1 28.2 %all-to-all-start = ((bf16[32,32,256]{2,1,0:T(8,128)(2,1)}), bf16[32,32,256]{2,1,0:T(8,128)(2,1)}, u32[]{:S(2)}, u32[]{:S(2)}) async-start(bf16[32,32,256]{2,1,0:T(8,128)(2,1)} %bitcast.42), calls=%async_computation | async-start | bytes 1048576 | tf_op jit(solution)/shard_map/all_to_all | solution.py:273
  59.3 8.6 %copy-start.2 = (bf16[2,512,512]{2,1,0:T(8,128)(2,1)S(1)}, bf16[2,512,512]{2,1,0:T(8,128)(2,1)}, u32[]{:S(2)}) copy-start(bf16[2,512,512]{2,1,0:T(8,128)(2,1)} %get-tuple-element.21) | copy-start | bytes 3145732
  69.0 16.6 %collective-permute-start.5 = (bf16[512,512]{1,0:T(8,128)(2,1)}, bf16[512,512]{1,0:T(8,128)(2,1)}, u32[]{:S(2)}, u32[]{:S(2)}) collective-permute-start(bf16[512,512]{1,0:T(8,128)(2,1)} %get-tuple-element.25), channel_id=1, source_target_pairs={{0,124},{4,0},{8,4},{12,8},{16,12},{20,16},{24,20},{28,24},{32,28}... | collective-permute-start | bytes 1572872 | tf_op jit(solution)/shard_map/ppermute | solution.py:16
  74.3 17.4 %collective-permute-start.6 = (bf16[512,512]{1,0:T(8,128)(2,1)}, bf16[512,512]{1,0:T(8,128)(2,1)}, u32[]{:S(2)}, u32[]{:S(2)}) collective-permute-start(bf16[512,512]{1,0:T(8,128)(2,1)} %get-tuple-element.26), channel_id=1, source_target_pairs={{0,4},{4,8},{8,12},{12,16},{16,20},{20,24},{24,28},{28,32},{32,36}... | collective-permute-start | bytes 1572872 | tf_op jit(solution)/shard_map/ppermute | solution.py:16
  77.4 8.2 %copy-start.3 = (bf16[2,512,512]{2,1,0:T(8,128)(2,1)S(1)}, bf16[2,512,512]{2,1,0:T(8,128)(2,1)}, u32[]{:S(2)}) copy-start(bf16[2,512,512]{2,1,0:T(8,128)(2,1)} %get-tuple-element.21) | copy-start | bytes 3145732
  77.8 22.2 %collective-permute-start.4 = (bf16[1024,256]{1,0:T(8,128)(2,1)S(1)}, bf16[1024,256]{1,0:T(8,128)(2,1)S(1)}, u32[]{:S(2)}, u32[]{:S(2)}) collective-permute-start(bf16[1024,256]{1,0:T(8,128)(2,1)S(1)} %fusion.2), channel_id=1, source_target_pairs={{0,2},{2,0},{1,3},{3,1},{4,6},{6,4},{5,7},{7,5},{8,10},{10,8},{9,1... | collective-permute-start | bytes 1572872 | tf_op jit(solution)/shard_map/ppermute | solution.py:24
  86.7 5.3 %copy-start.5 = (f32[1024,256]{1,0:T(8,128)S(1)}, f32[1024,256]{1,0:T(8,128)}, u32[]{:S(2)}) copy-start(f32[1024,256]{1,0:T(8,128)} %get-tuple-element.20) | copy-start | bytes 3145732
  86.7 5.3 %copy-start.6 = (f32[1024,256]{1,0:T(8,128)S(1)}, f32[1024,256]{1,0:T(8,128)}, u32[]{:S(2)}) copy-start(f32[1024,256]{1,0:T(8,128)} %get-tuple-element.22) | copy-start | bytes 3145732

commit v2 on v1

v2 whole, which is shorter than its diff:
```python
import jax
import jax.numpy as jnp
from jax import lax
from jax.experimental import pallas as pl
from jax.experimental.pallas import tpu as pltpu
from jax.sharding import PartitionSpec as P

HD = 64
T = 128
F32 = jnp.float32
BF16 = jnp.bfloat16


def ring(x, by):
    n = lax.axis_size("tm")
    return lax.ppermute(x, "tm", [(i, (i + by) % n) for i in range(n)])


def core_swap(x):
    return lax.ppermute(x, "head", [(0, 1), (1, 0), (2, 3), (3, 2)])


def chip_swap(x):
    return lax.ppermute(x, "head", [(0, 2), (2, 0), (1, 3), (3, 1)])


def nt(a, b):
    return lax.dot_general(a, b, (((1,), (1,)), ((), ())), preferred_element_type=F32)


def nn(a, b):
    return jnp.dot(a, b, preferred_element_type=F32)


def pair_stack(x):
    first = lax.broadcasted_iota(jnp.int32, x.shape, 1) < HD
    zero = jnp.zeros_like(x)
    return jnp.concatenate([jnp.where(first, x, zero), jnp.where(first, zero, x)], axis=0)


def own_blocks(x):
    return jnp.concatenate([x[:HD, :T], x[HD:, T:]], axis=0)


def per_head(r):
    return jnp.concatenate(
        [jnp.broadcast_to(r[:, :T], (HD, T)), jnp.broadcast_to(r[:, T:], (HD, T))], axis=0
    )


def head_sums(x):
    return jnp.concatenate(
        [jnp.sum(x[:HD], axis=0, keepdims=True), jnp.sum(x[HD:], axis=0, keepdims=True)], axis=1
    )


def listed(lists, row, tile):
    hit = lists[row, 0] == tile
    for c in range(1, lists.shape[1]):
        hit = hit | (lists[row, c] == tile)
    return jnp.where(hit & (tile >= 0), 1, 0)


def masked_max(s, oks, start):
    m = start
    for w, ok in enumerate(oks):
        mw = jnp.max(s[w * T : (w + 1) * T], axis=0, keepdims=True)
        mw = jnp.where(ok > 0, mw, -1e30)
        m = mw if m is None else jnp.maximum(m, mw)
    return m


def masked_exp(s, oks, m):
    parts, total = [], None
    for w, ok in enumerate(oks):
        p = jnp.exp(s[w * T : (w + 1) * T] - jnp.where(ok > 0, m, 1e30))
        t = jnp.sum(p, axis=0, keepdims=True)
        total = t if total is None else total + t
        parts.append(p.astype(BF16))
    return jnp.concatenate(parts, axis=0), total


def first_tile(where, half, n_tile):
    return (where[0] if half == 0 else 2 * where[1] - 1 - where[0]) * n_tile


def staged(items, stages):
    held = [dict() for _ in items]
    for step in range(len(items) + len(stages) - 1):
        for lag, stage in enumerate(stages):
            if 0 <= step - lag < len(items):
                stage(held[step - lag], *items[step - lag])


def chains(pairs, n_tile):
    return [(half, j, i) for half in range(2) for j in range(n_tile) for i in range(pairs)]


def lanes(i):
    return slice(2 * HD * i, 2 * HD * (i + 1))


def cols(j):
    return slice(2 * T * j, 2 * T * (j + 1))


def own_forward_kernel(where, lists, q, k, v, p_o, st_o, o_o, vt):
    pairs = q.shape[1] // (2 * HD)
    span = k.shape[0] // 2
    n_tile = span // T
    vt[...] = v[...].T
    key = lax.broadcasted_iota(jnp.int32, (T, 2 * T), 0)
    qry = lax.broadcasted_iota(jnp.int32, (T, 2 * T), 1) % T
    causal = key <= qry
    tile0 = [first_tile(where, half, n_tile) for half in range(2)]
    oks = [
        [[listed(lists, half * n_tile + j, tile0[half] + w) for w in range(j + 1)] for j in range(n_tile)]
        for half in range(2)
    ]

    def scores(d, half, j, i):
        lo = half * span
        row = lo + j * T
        qm = pair_stack(q[row : row + T, lanes(i)] * BF16(HD**-0.5))
        s = nt(k[lo : row + T, lanes(i)], qm)
        diag = jnp.where(causal, s[j * T :], -1e30)
        d["s"] = diag if j == 0 else jnp.concatenate([s[: j * T], diag], axis=0)

    def softmax(d, half, j, i):
        row = half * n_tile + j
        m = masked_max(d["s"], oks[half][j], None)
        d["p"], total = masked_exp(d.pop("s"), oks[half][j], m)
        p_o[half, i, : (j + 1) * T, cols(j)] = d["p"]
        st_o[row, 0:1, cols(i)] = m
        st_o[row, 1:2, cols(i)] = total

    def mix(d, half, j, i):
        lo = half * span
        row = lo + j * T
        o_o[lanes(i), row : row + T] = own_blocks(nn(vt[lanes(i), lo : row + T], d.pop("p")))

    staged(chains(pairs, n_tile), [scores, softmax, mix])


def halo_kernel(
    where, lists, q, k, v, kvu, kvd, ga, st, o1, att_o, attt_o, g_o, del_o, ret_o, dq_o, kp, vp, kt, vt, ps, ds, qs, gs
):
    pairs = q.shape[1] // (2 * HD)
    span = k.shape[0] // 2
    n_tile = span // T
    is_last = where[0] == where[1] - 1
    for half in range(2):
        if half == 0:
            kp[half] = kvu[:span]
            vp[half] = kvu[span:]
        else:
            kp[half] = jnp.where(is_last, k[:span], kvd[:span])
            vp[half] = jnp.where(is_last, v[:span], kvd[span:])
        kt[half] = kp[half].T
        vt[half] = vp[half].T
    tile0 = [first_tile(where, half, n_tile) - n_tile for half in range(2)]
    oks = [
        [[listed(lists, half * n_tile + j, tile0[half] + w) for w in range(j, n_tile)] for j in range(n_tile)]
        for half in range(2)
    ]

    def scores(d, half, j, i):
        row = half * span + j * T
        qm = pair_stack(q[row : row + T, lanes(i)] * BF16(HD**-0.5))
        qs[half, i, cols(j)] = qm
        d["s"] = nt(kp[half, j * T :, lanes(i)], qm)

    def softmax(d, half, j, i):
        row = half * n_tile + j
        m1 = st[row, 0:1, cols(i)]
        m = masked_max(d["s"], oks[half][j], m1)
        d["alpha"] = jnp.exp(m1 - m)
        d["p"], total = masked_exp(d.pop("s"), oks[half][j], m)
        ps[half, i, j * T :, cols(j)] = d["p"]
        d["inv"] = 1.0 / (d["alpha"] * st[row, 1:2, cols(i)] + total)

    def mix(d, half, j, i):
        d["o"] = own_blocks(nn(vt[half, lanes(i), j * T :], d.pop("p")))

    def finish(d, half, j, i):
        row = half * n_tile + j
        rows = slice(row * T, (row + 1) * T)
        alpha, inv = d.pop("alpha"), d.pop("inv")
        at = ((o1[lanes(i), rows] * per_head(alpha) + d.pop("o")) * per_head(inv)).astype(BF16)
        gh = ga[lanes(i), rows]
        g2 = (gh * per_head(inv)).astype(BF16)
        g1 = (gh * per_head(inv * alpha)).astype(BF16)
        af = at.astype(F32)
        d["d2"] = head_sums(af * g2.astype(F32))
        del_o[row, :, cols(i)] = head_sums(af * g1.astype(F32))
        attt_o[lanes(i), rows] = at
        att_o[rows, lanes(i)] = at.T
        g_o[rows, lanes(i)] = g1.T
        d["gm"] = pair_stack(g2.T)
        gs[half, i, cols(j)] = d["gm"]

    def dprob(d, half, j, i):
        d["dp"] = nt(vp[half, j * T :, lanes(i)], d.pop("gm"))

    def dscore(d, half, j, i):
        p = ps[half, i, j * T :, cols(j)].astype(F32)
        ds[half, i, j * T :, cols(j)] = (p * (d.pop("dp") - d.pop("d2"))).astype(BF16)

    def gradients(half):
        for i in range(pairs):
            for t in range(n_tile):
                upto = slice(0, 2 * T * (t + 1))
                tile = slice(t * T, (t + 1) * T)
                ret_o[half, tile, lanes(i)] = nn(ds[half, i, tile, upto], qs[half, i, upto]).astype(BF16)
                back = slice(span + t * T, span + (t + 1) * T)
                ret_o[half, back, lanes(i)] = nn(ps[half, i, tile, upto], gs[half, i, upto]).astype(BF16)
            for j in range(n_tile):
                row = half * span + j * T
                dq_o[lanes(i), row : row + T] = own_blocks(
                    nn(kt[half, lanes(i), j * T :], ds[half, i, j * T :, cols(j)])
                )

    staged(chains(pairs, n_tile), [scores, softmax, mix, finish, dprob, dscore])
    for half in range(2):
        gradients(half)


def own_back_kernel(where, q, k, v, p, g, dl, dqp, ret, low, high, dq_o, dk_o, dv_o, kt, ds, qs, gs):
    pairs = q.shape[1] // (2 * HD)
    span = k.shape[0] // 2
    n_tile = span // T
    is_last = where[0] == where[1] - 1
    is_first = where[0] == 0
    kt[...] = k[...].T

    def dprob(d, half, j, i):
        lo = half * span
        row = lo + j * T
        gm = pair_stack(g[row : row + T, lanes(i)])
        gs[half, i, cols(j)] = gm
        qs[half, i, cols(j)] = pair_stack(q[row : row + T, lanes(i)] * BF16(HD**-0.5))
        d["dp"] = nt(v[lo : row + T, lanes(i)], gm)

    def dscore(d, half, j, i):
        size = (j + 1) * T
        pf = p[half, i, :size, cols(j)].astype(F32)
        ds[half, i, :size, cols(j)] = (pf * (d.pop("dp") - dl[half * n_tile + j, :, cols(i)])).astype(BF16)

    def gradients(half):
        lo = half * span
        for i in range(pairs):
            for t in range(n_tile):
                since = slice(2 * T * t, 2 * T * n_tile)
                tile = slice(t * T, (t + 1) * T)
                there = slice(span + t * T, span + (t + 1) * T)
                rows = slice(lo + t * T, lo + (t + 1) * T)
                dk = nn(ds[half, i, tile, since], qs[half, i, since])
                dv = nn(p[half, i, tile, since], gs[half, i, since])
                if half == 0:
                    hk = jnp.where(is_last, ret[1, tile, lanes(i)], low[tile, lanes(i)])
                    hv = jnp.where(is_last, ret[1, there, lanes(i)], low[there, lanes(i)])
                else:
                    hk, hv = high[tile, lanes(i)], high[there, lanes(i)]
                    hk = jnp.where(is_first, jnp.zeros_like(hk), hk)
                    hv = jnp.where(is_first, jnp.zeros_like(hv), hv)
                dk_o[rows, lanes(i)] = (dk + hk.astype(F32)).astype(BF16)
                dv_o[rows, lanes(i)] = (dv + hv.astype(F32)).astype(BF16)
            for j in range(n_tile):
                rows = slice(lo + j * T, lo + (j + 1) * T)
                dq = own_blocks(nn(kt[lanes(i), lo : lo + (j + 1) * T], ds[half, i, : (j + 1) * T, cols(j)]))
                dq_o[rows, lanes(i)] = ((dq + dqp[lanes(i), rows]) * HD**-0.5).astype(BF16).T

    staged(chains(pairs, n_tile), [dprob, dscore])
    for half in range(2):
        gradients(half)


def weight_kernel(at, go, w_o):
    w_o[...] = nn(at[...], go[...]).astype(BF16).T


def call(body, outs, scratch, scalars, flops, *args):
    vm = pl.BlockSpec(memory_space=pltpu.VMEM)
    sm = pl.BlockSpec(memory_space=pltpu.SMEM)
    return pl.pallas_call(
        body,
        out_shape=outs,
        in_specs=[sm] * scalars + [vm] * (len(args) - scalars),
        out_specs=[vm] * len(outs),
        scratch_shapes=scratch,
        compiler_params=pltpu.CompilerParams(vmem_limit_bytes=56 << 20),
        cost_estimate=pl.CostEstimate(flops=flops, transcendentals=0, bytes_accessed=8 << 20),
    )(*args)


def on_device(queries, keys, values, out_weight, grad_output, tile_lists):
    rows, width = queries.shape
    heads = width // HD
    span = rows // 2
    n_tile = span // T
    n_row = 2 * n_tile
    tm_count = lax.axis_size("tm")
    tm_index = lax.axis_index("tm")
    head_index = lax.axis_index("head")
    where = jnp.stack([tm_index, jnp.int32(tm_count)]).astype(jnp.int32)

    def arr(dtype, *dims):
        return jax.ShapeDtypeStruct(dims, dtype)

    def vmem(dtype, *dims):
        return pltpu.VMEM(dims, dtype)

    kvu = ring(jnp.concatenate([keys[:span], values[:span]], axis=0), 1)
    kvd = ring(jnp.concatenate([keys[span:], values[span:]], axis=0), -1)

    w4 = out_weight.reshape(width, 2, 2, width)
    core = head_index % 2
    chip = head_index // 2
    w_core = lax.dynamic_index_in_dim(w4, core, axis=2, keepdims=False)
    w_send = lax.dynamic_index_in_dim(w4, 1 - core, axis=2, keepdims=False)
    w_recv = core_swap(w_send.reshape(width, 2 * width)).reshape(width, 2, width)

    ga = lax.dot_general(out_weight, grad_output, (((1,), (1,)), ((), ())), preferred_element_type=F32)

    p, st, o1 = call(
        own_forward_kernel,
        [arr(BF16, 2, heads // 2, span, 2 * span), arr(F32, n_row, 2, heads * T), arr(F32, width, rows)],
        [vmem(BF16, width, rows)],
        2,
        10**9,
        where,
        tile_lists,
        queries,
        keys,
        values,
    )
    att, at, g, dl, ret, dqp = call(
        halo_kernel,
        [
            arr(BF16, rows, width),
            arr(BF16, width, rows),
            arr(BF16, rows, width),
            arr(F32, n_row, 1, heads * T),
            arr(BF16, 2, rows, width),
            arr(F32, width, rows),
        ],
        [vmem(BF16, 2, span, width)] * 2
        + [vmem(BF16, 2, width, span)] * 2
        + [vmem(BF16, 2, heads // 2, span, 2 * span)] * 2
        + [vmem(BF16, 2, heads // 2, 2 * span, 2 * HD)] * 2,
        2,
        4 * 10**9,
        where,
        tile_lists,
        queries,
        keys,
        values,
        kvu,
        kvd,
        ga,
        st,
        o1,
    )
    low = ring(ret[0], -1)
    high = ring(ret[1], 1)

    att_other = core_swap(att)
    (w_mine,) = call(weight_kernel, [arr(BF16, grad_output.shape[1], width)], [], 0, 10**9, at, grad_output)
    there = lax.dynamic_index_in_dim(w_core, 1 - chip, axis=1, keepdims=False)
    there_o = lax.dynamic_index_in_dim(w_recv, 1 - chip, axis=1, keepdims=False)
    here = lax.dynamic_index_in_dim(w_core, chip, axis=1, keepdims=False)
    here_o = lax.dynamic_index_in_dim(w_recv, chip, axis=1, keepdims=False)
    out_recv = chip_swap((nn(att, there) + nn(att_other, there_o)).astype(BF16))
    w_parts = lax.all_to_all(w_mine.reshape(tm_count, -1, width), "tm", 0, 0, tiled=True)

    dq, dk, dv = call(
        own_back_kernel,
        [arr(BF16, rows, width)] * 3,
        [vmem(BF16, width, rows), vmem(BF16, 2, heads // 2, span, 2 * span)]
        + [vmem(BF16, 2, heads // 2, 2 * span, 2 * HD)] * 2,
        1,
        4 * 10**9,
        where,
        queries,
        keys,
        values,
        p,
        g,
        dl,
        dqp,
        ret,
        low,
        high,
    )
    output = (nn(att, here) + nn(att_other, here_o) + out_recv.astype(F32)).astype(BF16)
    scale = (tm_count * rows) ** -0.5
    grad_weight = (jnp.sum(w_parts.astype(F32), axis=0) * scale).T
    return output, dq, dk, dv, grad_weight


def solution(mesh):
    return jax.shard_map(
        on_device,
        mesh=mesh,
        in_specs=(
            P("tm", "head"),
            P("tm", "head"),
            P("tm", "head"),
            P("head", None),
            P("tm", None),
            P("tm", None),
        ),
        out_specs=(
            P("tm", "head"),
            P("tm", "head"),
            P("tm", "head"),
            P("tm", "head"),
            P("head", "tm"),
        ),
        check_vma=False,
    )
```

time: 102 us -> 81.9 us (0.80)
  waiting for transfers between devices: 28.3 us -> 21.9 us
  matrix products: 8.61 us -> 3.89 us
  local copies, waits for them, and re-layouts: 7.38 us -> 3.47 us
  other arithmetic: 5 us -> 2.23 us
  Pallas kernels: 27.6 us -> 26.1 us
  starting transfers between devices: 23.4 us -> 22.3 us
    ppermute x1, waiting for transfers between devices: 6.66 us -> 0.62 us  [chip_swap(): return lax.ppermute(x, 'head', [(0, 2), (2, 0), (1, 3), (3, 1)])]
    dot_general x1 -> x0, matrix products: 2.65 us -> none  [on_device(): lax.dot_general(grad_output, att, (((0,), (0,)), ((), ())), preferred_ele...]
    dot_general x4, matrix products: 4.21 us -> 2.13 us  [nn(): return jnp.dot(a, b, preferred_element_type=F32)]
    convert_element_type x1 -> x0, local copies, waits for them, and re-layouts: 2.04 us -> none  [on_device(): w_split = wt.astype(BF16).reshape(tm_count, -1, width)]
    pallas_call x3 -> x4, Pallas kernels: 27.6 us -> 26.1 us  [call(): pl.pallas_call(body, out_shape=outs, in_specs=[sm] * scalars + [vm] * (le...]
    unnamed x16 -> x7, local copies, waits for them, and re-layouts: 1.47 us -> 0.21 us
    convert_element_type x1 -> x0, other arithmetic: 1.2 us -> none  [on_device(): grad_values = (dv + halo[:, width:]).astype(BF16)]
    select_n x2 -> x0, other arithmetic: 1.14 us -> none  [the longest x1 1.1 us: on_device(): low = jnp.where(is_last, ret[1], back_low).astype(F32)]
  transfers between devices with their start and end apart: 8 -> 8, of which waited for: 5 -> 5; matrix products, arithmetic and copies ran while one was open for 16% -> 9% of each run, Pallas kernels for 27% -> 17%
where the time goes in v2:
time: 81.9 us; the launch traced here: 80.7 us
  Pallas kernels  26.1 us (32%)
  starting transfers between devices  22.3 us (27%)
  waiting for transfers between devices  21.9 us (27%)
  matrix products  3.89 us (5%)
  local copies, waits for them, and re-layouts  3.47 us (4%)
  other arithmetic  2.23 us (3%)
    pallas_call x4, Pallas kernels, call(): pl.pallas_call(body, out_shape=outs, in_specs=[sm] * scalars + [vm] * (le...  26.1 us
    ppermute x4, waiting for transfers between devices, ring(): return lax.ppermute(x, 'tm', [(i, (i + by) % n) for i in range(n)])  21.3 us
    ppermute x4, starting transfers between devices, ring(): return lax.ppermute(x, 'tm', [(i, (i + by) % n) for i in range(n)])  13.9 us
    all_to_all x1, starting transfers between devices, on_device(): lax.all_to_all(w_mine.reshape(tm_count, -1, width), 'tm', 0, 0, tiled=True)  4.02 us
    ppermute x1, starting transfers between devices, chip_swap(): return lax.ppermute(x, 'head', [(0, 2), (2, 0), (1, 3), (3, 1)])  2.53 us
    dot_general x4, matrix products, nn(): return jnp.dot(a, b, preferred_element_type=F32)  2.13 us
    ppermute x2, starting transfers between devices, core_swap(): return lax.ppermute(x, 'head', [(0, 1), (1, 0), (2, 3), (3, 2)])  1.87 us
    dot_general x1, matrix products, on_device(): lax.dot_general(out_weight, grad_output, (((1,), (1,)), ((), ())), prefer...  1.76 us
  transfers between devices with their start and end apart: 8, of which 5 were waited for; matrix products, arithmetic and copies ran while one was open for 9% of the time, Pallas kernels for 17%

profile of v2, /device:TPU:1, one launch (start us, length us, event | category | flops | bytes accessed | tf_op | source)
XLA Modules:
  0.0 80.7 jit_solution(16609814858997991049)
XLA Ops:
  0.6 1.3 %fusion.17 = (bf16[512,256]{1,0:T(8,128)(2,1)S(1)}, bf16[512,256]{1,0:T(8,128)(2,1)S(1)}, bf16[512,256]{1,0:T(8,128)(2,1)S(1)}, bf16[512,256]{1,0:T(8,128)(2,1)S(1)}) fusion(bf16[1024,256]{1,0:T(8,128)(2,1)} %k.5, bf16[1024,256]{1,0:T(8,128)(2,1)} %v.5), kind=kLoop, calls=%fused_computation.27 | loop fusion | bytes 2097152 | tf_op jit(solution)/shard_map/slice | solution.py:314
  1.9 8.0 %collective-permute-start.1 = (bf16[1024,256]{1,0:T(8,128)(2,1)S(1)}, bf16[1024,256]{1,0:T(8,128)(2,1)}, u32[]{:S(2)}, u32[]{:S(2)}) collective-permute-start(bf16[1024,256]{1,0:T(8,128)(2,1)S(1)} %pad_maximum_fusion.1), channel_id=1, source_target_pairs={{0,124},{4,0},{8,4},{12,8},{16,12},{20,16},{24,20},{28,24},{32,28}... | collective-permute-start | bytes 1572872 | tf_op jit(solution)/shard_map/ppermute | solution.py:16
  10.0 0.8 %pad_maximum_fusion = bf16[1024,256]{1,0:T(8,128)(2,1)} fusion(bf16[512,256]{1,0:T(8,128)(2,1)S(1)} %get-tuple-element.35, bf16[512,256]{1,0:T(8,128)(2,1)S(1)} %get-tuple-element.32), kind=kLoop, calls=%fused_computation.6 | loop fusion | flops 1048576 | bytes 1048576 | tf_op jit(solution)/shard_map/concatenate | solution.py:313
  10.8 0.0 copy-start
  10.8 0.0 copy-start.1
  10.8 0.0 collective-permute-start
  10.8 0.7 pad_add_fusion.where
  11.5 6.0 %shard_map.101 = (bf16[2,2,512,1024]{3,2,1,0:T(8,128)(2,1)}, f32[8,2,512]{2,1,0:T(2,128)}, f32[256,1024]{1,0:T(8,128)}) custom-call(s32[2]{0:T(128)} %pad_add_fusion.where, s32[8,5]{1,0:T(8,128)} %lists.3, bf16[1024,256]{1,0:T(8,128)(2,1)} %q.5, bf16[1024,256]{1,0:T(8,128)(2,1)} %k.5, bf16[1024,256]{1,0:T(8,128)(2,1)} %v.5), custom_call_target="tpu_custom_call" | custom-call | flops 1000000000 | bytes 8388608 | tf_op jit(solution)/shard_map/pallas_call | solution.py:285
  17.5 0.0 copy-done
  17.5 0.0 copy-done.1
  17.5 1.8 %fusion.19.ga = f32[256,1024]{1,0:T(8,128)} fusion(bf16[256,1024]{1,0:T(8,128)(2,1)S(1)} %copy-done.1, bf16[1024,1024]{1,0:T(8,128)(2,1)S(1)} %copy-done), kind=kOutput, calls=%fused_computation.29 | convolution fusion | flops 536870912 | bytes 3670016 | tf_op jit(solution)/shard_map/dot_general | solution.py:323
  19.2 1.3 %collective-permute-done.1.kvd = bf16[1024,256]{1,0:T(8,128)(2,1)} collective-permute-done((bf16[1024,256]{1,0:T(8,128)(2,1)S(1)}, bf16[1024,256]{1,0:T(8,128)(2,1)}, u32[]{:S(2)}, u32[]{:S(2)}) %collective-permute-start.1) | collective-permute-done | bytes 524320 | tf_op jit(solution)/shard_map/ppermute | solution.py:16
  20.6 7.2 %collective-permute-done.kvu = bf16[1024,256]{1,0:T(8,128)(2,1)} collective-permute-done((bf16[1024,256]{1,0:T(8,128)(2,1)}, bf16[1024,256]{1,0:T(8,128)(2,1)}, u32[]{:S(2)}, u32[]{:S(2)}) %collective-permute-start) | collective-permute-done | bytes 524320 | tf_op jit(solution)/shard_map/ppermute | solution.py:16
  27.8 9.2 %shard_map.102 = (bf16[1024,256]{1,0:T(8,128)(2,1)}, bf16[256,1024]{1,0:T(8,128)(2,1)}, bf16[1024,256]{1,0:T(8,128)(2,1)}, f32[8,1,512]{2,1,0:T(1,128)}, bf16[2,...) custom-call(s32[2]{0:T(128)} %pad_add_fusion.where, s32[8,5]{1,0:T(8,128)} %lists.3, bf16[1024,256]{1,0:T(8,128)(2,1)} %q.5, ...), custom_call_target="tpu_custom_call" | custom-call | flops 4000000000 | bytes 8388608 | tf_op jit(solution)/shard_map/pallas_call | solution.py:285
  37.0 3.3 %shard_map.104 = bf16[1024,256]{1,0:T(8,128)(2,1)} custom-call(bf16[256,1024]{1,0:T(8,128)(2,1)} %get-tuple-element.28.at, bf16[1024,1024]{1,0:T(8,128)(2,1)} %go.1), custom_call_target="tpu_custom_call" | custom-call | flops 1000000000 | bytes 8388608 | tf_op jit(solution)/shard_map/pallas_call | solution.py:285
  40.3 0.0 copy-start.2
  40.3 4.0 %all-to-all-start = ((bf16[32,32,256]{2,1,0:T(8,128)(2,1)}), bf16[32,32,256]{2,1,0:T(8,128)(2,1)S(1)}, u32[]{:S(2)}, u32[]{:S(2)}) async-start(bf16[32,32,256]{2,1,0:T(8,128)(2,1)} %bitcast.36), calls=%async_computation | async-start | bytes 1048576 | tf_op jit(solution)/shard_map/all_to_all | solution.py:374
  44.4 0.2 copy.14
  44.6 0.7 constant_dynamic-slice_fusion
  45.3 1.9 %collective-permute-start.3 = (bf16[256,512]{0,1:T(8,128)(2,1)}, bf16[256,512]{0,1:T(8,128)(2,1)S(1)}, u32[]{:S(2)}, u32[]{:S(2)}) collective-permute-start(bf16[256,512]{0,1:T(8,128)(2,1)} %bitcast.3), channel_id=1, source_target_pairs={{0,1},{1,0},{2,3},{3,2},{4,5},{5,4},{6,7},{7,6},{8,9},{9,8},{10,11... | collective-permute-start | bytes 786440 | tf_op jit(solution)/shard_map/ppermute | solution.py:20
  47.2 0.0 copy-done.2
  47.2 0.0 collective-permute-start.2
  47.2 1.3 %slice_bitcast_fusion = (bf16[1024,256]{1,0:T(8,128)(2,1)S(1)}, bf16[1024,256]{1,0:T(8,128)(2,1)S(1)}) fusion(bf16[2,1024,256]{2,1,0:T(8,128)(2,1)} %get-tuple-element.24.ret), kind=kLoop, calls=%fused_computation.8 | loop fusion | bytes 2097152 | tf_op jit(solution)/shard_map/squeeze | solution.py:365
  48.5 5.9 %collective-permute-start.5 = (bf16[1024,256]{1,0:T(8,128)(2,1)S(1)}, bf16[1024,256]{1,0:T(8,128)(2,1)}, u32[]{:S(2)}, u32[]{:S(2)}) collective-permute-start(bf16[1024,256]{1,0:T(8,128)(2,1)S(1)} %get-tuple-element.30), channel_id=1, source_target_pairs={{0,124},{4,0},{8,4},{12,8},{16,12},{20,16},{24,20},{28,24},{32,28}... | collective-permute-start | bytes 1572872 | tf_op jit(solution)/shard_map/ppermute | solution.py:16
  54.3 0.0 collective-permute-start.6
  54.4 0.0 all-to-all-done
  54.4 0.1 convert_reduce_fusion
  54.4 0.6 multiply_bitcast_fusion
  55.1 0.0 collective-permute-done.3
  55.1 0.0 collective-permute-done.2
  55.1 0.3 fusion.3
  55.4 0.3 fusion.2
  55.8 2.5 %collective-permute-start.4 = (bf16[1024,256]{1,0:T(8,128)(2,1)S(1)}, bf16[1024,256]{1,0:T(8,128)(2,1)S(1)}, u32[]{:S(2)}, u32[]{:S(2)}) collective-permute-start(bf16[1024,256]{1,0:T(8,128)(2,1)S(1)} %fusion.2), channel_id=1, source_target_pairs={{0,2},{2,0},{1,3},{3,1},{4,6},{6,4},{5,7},{7,5},{8,10},{10,8},{9,1... | collective-permute-start | bytes 1572872 | tf_op jit(solution)/shard_map/ppermute | solution.py:24
  58.3 0.3 fusion.6
  58.6 6.5 %collective-permute-done.5.low = bf16[1024,256]{1,0:T(8,128)(2,1)} collective-permute-done((bf16[1024,256]{1,0:T(8,128)(2,1)S(1)}, bf16[1024,256]{1,0:T(8,128)(2,1)}, u32[]{:S(2)}, u32[]{:S(2)}) %collective-permute-start.5) | collective-permute-done | bytes 524320 | tf_op jit(solution)/shard_map/ppermute | solution.py:16
  65.1 6.2 %collective-permute-done.6.high = bf16[1024,256]{1,0:T(8,128)(2,1)} collective-permute-done((bf16[1024,256]{1,0:T(8,128)(2,1)S(1)}, bf16[1024,256]{1,0:T(8,128)(2,1)}, u32[]{:S(2)}, u32[]{:S(2)}) %collective-permute-start.6) | collective-permute-done | bytes 524320 | tf_op jit(solution)/shard_map/ppermute | solution.py:16
  71.3 7.6 %shard_map.103 = (bf16[1024,256]{1,0:T(8,128)(2,1)}, bf16[1024,256]{1,0:T(8,128)(2,1)}, bf16[1024,256]{1,0:T(8,128)(2,1)}) custom-call(s32[2]{0:T(128)} %pad_add_fusion.where, bf16[1024,256]{1,0:T(8,128)(2,1)} %q.5, bf16[1024,256]{1,0:T(8,128)(2,1)} %k.5, bf16[1024,256]{1,0:T(8,128)(2,1)} %v.5, bf16[2,2,512,1024]{3,2,1,0:T(8,128)(2,1)} %get-tuple-element.20.p, ...), custom_call_target="tpu_custom_call" | custom-call | flops 4000000000 | bytes 8388608 | tf_op jit(solution)/shard_map/pallas_call | solution.py:285
  78.9 0.6 collective-permute-done.4
  79.5 1.1 %fusion.1 = bf16[1024,256]{1,0:T(8,128)(2,1)} fusion(f32[1024,256]{1,0:T(8,128)S(1)} %fusion.6, bf16[1024,256]{1,0:T(8,128)(2,1)S(1)} %copy-done.2, bf16[1024,256]{1,0:T(8,128)(2,1)S(1)} %collective-permute-done.4, bf16[256,2,2,256]{0,3,2,1:T(8,128)(2,1)S(1)} %bitcast.35, s32[]{:T(128)S(6)} %select_n.35, s32[]{:T(128)S(6)} %select_n.38), kind=kOutput, calls=%fused_computation.3 | convolution fusion | flops 135266304 | bytes 2752520 | tf_op jit(solution)/shard_map/dot_general | solution.py:32
  (1 shorter events, 0.0 us)
Async XLA Ops:
  1.9 18.6 %collective-permute-start.1 = (bf16[1024,256]{1,0:T(8,128)(2,1)S(1)}, bf16[1024,256]{1,0:T(8,128)(2,1)}, u32[]{:S(2)}, u32[]{:S(2)}) collective-permute-start(bf16[1024,256]{1,0:T(8,128)(2,1)S(1)} %pad_maximum_fusion.1), channel_id=1, source_target_pairs={{0,124},{4,0},{8,4},{12,8},{16,12},{20,16},{24,20},{28,24},{32,28}... | collective-permute-start | bytes 1572872 | tf_op jit(solution)/shard_map/ppermute | solution.py:16
  10.8 6.7 %copy-start = (bf16[1024,1024]{1,0:T(8,128)(2,1)S(1)}, bf16[1024,1024]{1,0:T(8,128)(2,1)}, u32[]{:S(2)}) copy-start(bf16[1024,1024]{1,0:T(8,128)(2,1)} %go.1) | copy-start | bytes 6291460
  10.8 6.7 %copy-start.1 = (bf16[256,1024]{1,0:T(8,128)(2,1)S(1)}, bf16[256,1024]{1,0:T(8,128)(2,1)}, u32[]{:S(2)}) copy-start(bf16[256,1024]{1,0:T(8,128)(2,1)} %param.9) | copy-start | bytes 1572868
  10.8 17.0 %collective-permute-start = (bf16[1024,256]{1,0:T(8,128)(2,1)}, bf16[1024,256]{1,0:T(8,128)(2,1)}, u32[]{:S(2)}, u32[]{:S(2)}) collective-permute-start(bf16[1024,256]{1,0:T(8,128)(2,1)} %pad_maximum_fusion), channel_id=1, source_target_pairs={{0,4},{4,8},{8,12},{12,16},{16,20},{20,24},{24,28},{28,32},{32,36}... | collective-permute-start | bytes 1572872 | tf_op jit(solution)/shard_map/ppermute | solution.py:16
  40.3 6.9 %copy-start.2 = (bf16[1024,256]{1,0:T(8,128)(2,1)S(1)}, bf16[1024,256]{1,0:T(8,128)(2,1)}, u32[]{:S(2)}) copy-start(bf16[1024,256]{1,0:T(8,128)(2,1)} %get-tuple-element.19) | copy-start | bytes 1572868
  40.3 14.0 %all-to-all-start = ((bf16[32,32,256]{2,1,0:T(8,128)(2,1)}), bf16[32,32,256]{2,1,0:T(8,128)(2,1)S(1)}, u32[]{:S(2)}, u32[]{:S(2)}) async-start(bf16[32,32,256]{2,1,0:T(8,128)(2,1)} %bitcast.36), calls=%async_computation | async-start | bytes 1048576 | tf_op jit(solution)/shard_map/all_to_all | solution.py:374
  45.3 9.7 %collective-permute-start.3 = (bf16[256,512]{0,1:T(8,128)(2,1)}, bf16[256,512]{0,1:T(8,128)(2,1)S(1)}, u32[]{:S(2)}, u32[]{:S(2)}) collective-permute-start(bf16[256,512]{0,1:T(8,128)(2,1)} %bitcast.3), channel_id=1, source_target_pairs={{0,1},{1,0},{2,3},{3,2},{4,5},{5,4},{6,7},{7,6},{8,9},{9,8},{10,11... | collective-permute-start | bytes 786440 | tf_op jit(solution)/shard_map/ppermute | solution.py:20
  47.2 7.9 %collective-permute-start.2 = (bf16[1024,256]{1,0:T(8,128)(2,1)S(1)}, bf16[1024,256]{1,0:T(8,128)(2,1)S(1)}, u32[]{:S(2)}, u32[]{:S(2)}) collective-permute-start(bf16[1024,256]{1,0:T(8,128)(2,1)S(1)} %copy-done.2), channel_id=1, source_target_pairs={{0,1},{1,0},{2,3},{3,2},{4,5},{5,4},{6,7},{7,6},{8,9},{9,8},{10,11... | collective-permute-start | bytes 1572872 | tf_op jit(solution)/shard_map/ppermute | solution.py:20
  48.5 16.7 %collective-permute-start.5 = (bf16[1024,256]{1,0:T(8,128)(2,1)S(1)}, bf16[1024,256]{1,0:T(8,128)(2,1)}, u32[]{:S(2)}, u32[]{:S(2)}) collective-permute-start(bf16[1024,256]{1,0:T(8,128)(2,1)S(1)} %get-tuple-element.30), channel_id=1, source_target_pairs={{0,124},{4,0},{8,4},{12,8},{16,12},{20,16},{24,20},{28,24},{32,28}... | collective-permute-start | bytes 1572872 | tf_op jit(solution)/shard_map/ppermute | solution.py:16
  54.3 17.0 %collective-permute-start.6 = (bf16[1024,256]{1,0:T(8,128)(2,1)S(1)}, bf16[1024,256]{1,0:T(8,128)(2,1)}, u32[]{:S(2)}, u32[]{:S(2)}) collective-permute-start(bf16[1024,256]{1,0:T(8,128)(2,1)S(1)} %get-tuple-element.29), channel_id=1, source_target_pairs={{0,4},{4,8},{8,12},{12,16},{16,20},{20,24},{24,28},{28,32},{32,36}... | collective-permute-start | bytes 1572872 | tf_op jit(solution)/shard_map/ppermute | solution.py:16
  55.8 23.8 %collective-permute-start.4 = (bf16[1024,256]{1,0:T(8,128)(2,1)S(1)}, bf16[1024,256]{1,0:T(8,128)(2,1)S(1)}, u32[]{:S(2)}, u32[]{:S(2)}) collective-permute-start(bf16[1024,256]{1,0:T(8,128)(2,1)S(1)} %fusion.2), channel_id=1, source_target_pairs={{0,2},{2,0},{1,3},{3,1},{4,6},{6,4},{5,7},{7,5},{8,10},{10,8},{9,1... | collective-permute-start | bytes 1572872 | tf_op jit(solution)/shard_map/ppermute | solution.py:24

commit v3 on v2

--- a/solution.py
+++ b/solution.py
@@ -143,7 +143,7 @@
 
 
 def halo_kernel(
-    where, lists, q, k, v, kvu, kvd, ga, st, o1, att_o, attt_o, g_o, del_o, ret_o, dq_o, kp, vp, kt, vt, ps, ds, qs, gs
+    where, lists, q, k, v, kvu, kvd, ga, st, o1, att_o, attt_o, g_o, del_o, low_o, high_o, dq_o, kp, vp, kt, vt, ps, ds, qs, gs
 ):
     pairs = q.shape[1] // (2 * HD)
     span = k.shape[0] // 2
@@ -207,13 +207,14 @@
         ds[half, i, j * T :, cols(j)] = (p * (d.pop("dp") - d.pop("d2"))).astype(BF16)
 
     def gradients(half):
+        ret_o = low_o if half == 0 else high_o
         for i in range(pairs):
             for t in range(n_tile):
                 upto = slice(0, 2 * T * (t + 1))
                 tile = slice(t * T, (t + 1) * T)
-                ret_o[half, tile, lanes(i)] = nn(ds[half, i, tile, upto], qs[half, i, upto]).astype(BF16)
+                ret_o[tile, lanes(i)] = nn(ds[half, i, tile, upto], qs[half, i, upto]).astype(BF16)
                 back = slice(span + t * T, span + (t + 1) * T)
-                ret_o[half, back, lanes(i)] = nn(ps[half, i, tile, upto], gs[half, i, upto]).astype(BF16)
+                ret_o[back, lanes(i)] = nn(ps[half, i, tile, upto], gs[half, i, upto]).astype(BF16)
             for j in range(n_tile):
                 row = half * span + j * T
                 dq_o[lanes(i), row : row + T] = own_blocks(
@@ -257,8 +258,8 @@
                 dk = nn(ds[half, i, tile, since], qs[half, i, since])
                 dv = nn(p[half, i, tile, since], gs[half, i, since])
                 if half == 0:
-                    hk = jnp.where(is_last, ret[1, tile, lanes(i)], low[tile, lanes(i)])
-                    hv = jnp.where(is_last, ret[1, there, lanes(i)], low[there, lanes(i)])
+                    hk = jnp.where(is_last, ret[tile, lanes(i)], low[tile, lanes(i)])
+                    hv = jnp.where(is_last, ret[there, lanes(i)], low[there, lanes(i)])
                 else:
                     hk, hv = high[tile, lanes(i)], high[there, lanes(i)]
                     hk = jnp.where(is_first, jnp.zeros_like(hk), hk)
@@ -313,13 +314,6 @@
     kvu = ring(jnp.concatenate([keys[:span], values[:span]], axis=0), 1)
     kvd = ring(jnp.concatenate([keys[span:], values[span:]], axis=0), -1)
 
-    w4 = out_weight.reshape(width, 2, 2, width)
-    core = head_index % 2
-    chip = head_index // 2
-    w_core = lax.dynamic_index_in_dim(w4, core, axis=2, keepdims=False)
-    w_send = lax.dynamic_index_in_dim(w4, 1 - core, axis=2, keepdims=False)
-    w_recv = core_swap(w_send.reshape(width, 2 * width)).reshape(width, 2, width)
-
     ga = lax.dot_general(out_weight, grad_output, (((1,), (1,)), ((), ())), preferred_element_type=F32)
 
     p, st, o1 = call(
@@ -334,14 +328,27 @@
         keys,
         values,
     )
-    att, at, g, dl, ret, dqp = call(
+    st, weight = lax.optimization_barrier((st, out_weight))
+    w4 = weight.reshape(width, 2, 2, width)
+    core = head_index % 2
+    chip = head_index // 2
+    w_core = lax.dynamic_index_in_dim(w4, core, axis=2, keepdims=False)
+    w_send = lax.dynamic_index_in_dim(w4, 1 - core, axis=2, keepdims=False)
+    w_recv = core_swap(w_send.reshape(width, 2 * width)).reshape(width, 2, width)
+    there = lax.dynamic_index_in_dim(w_core, 1 - chip, axis=1, keepdims=False)
+    there_o = lax.dynamic_index_in_dim(w_recv, 1 - chip, axis=1, keepdims=False)
+    here = lax.dynamic_index_in_dim(w_core, chip, axis=1, keepdims=False)
+    here_o = lax.dynamic_index_in_dim(w_recv, chip, axis=1, keepdims=False)
+    st, here, here_o, there, there_o = lax.optimization_barrier((st, here, here_o, there, there_o))
+    att, at, g, dl, ret_low, ret_high, dqp = call(
         halo_kernel,
         [
             arr(BF16, rows, width),
             arr(BF16, width, rows),
             arr(BF16, rows, width),
             arr(F32, n_row, 1, heads * T),
-            arr(BF16, 2, rows, width),
+            arr(BF16, rows, width),
+            arr(BF16, rows, width),
             arr(F32, width, rows),
         ],
         [vmem(BF16, 2, span, width)] * 2
@@ -361,15 +368,12 @@
         st,
         o1,
     )
-    low = ring(ret[0], -1)
-    high = ring(ret[1], 1)
+    low = ring(ret_low, -1)
+    high = ring(ret_high, 1)
 
     att_other = core_swap(att)
+    at, att_other = lax.optimization_barrier((at, att_other))
     (w_mine,) = call(weight_kernel, [arr(BF16, grad_output.shape[1], width)], [], 0, 10**9, at, grad_output)
-    there = lax.dynamic_index_in_dim(w_core, 1 - chip, axis=1, keepdims=False)
-    there_o = lax.dynamic_index_in_dim(w_recv, 1 - chip, axis=1, keepdims=False)
-    here = lax.dynamic_index_in_dim(w_core, chip, axis=1, keepdims=False)
-    here_o = lax.dynamic_index_in_dim(w_recv, chip, axis=1, keepdims=False)
     out_recv = chip_swap((nn(att, there) + nn(att_other, there_o)).astype(BF16))
     w_parts = lax.all_to_all(w_mine.reshape(tm_count, -1, width), "tm", 0, 0, tiled=True)
 
@@ -388,7 +392,7 @@
         g,
         dl,
         dqp,
-        ret,
+        ret_high,
         low,
         high,
     )

time: 81.9 us -> 73.4 us (0.90); the launches traced: 80.7 us -> 73 us
  waiting for transfers between devices: 21.9 us -> 8.79 us
  starting transfers between devices: 22.3 us -> 26.4 us
  matrix products: 3.89 us -> 4.77 us
    ppermute x4, waiting for transfers between devices: 21.3 us -> 4.42 us  [ring(): return lax.ppermute(x, 'tm', [(i, (i + by) % n) for i in range(n)])]
    ppermute x1, waiting for transfers between devices: 0.62 us -> 4.36 us  [chip_swap(): return lax.ppermute(x, 'head', [(0, 2), (2, 0), (1, 3), (3, 1)])]
    all_to_all x1, starting transfers between devices: 4.02 us -> 7.66 us  [on_device(): lax.all_to_all(w_mine.reshape(tm_count, -1, width), 'tm', 0, 0, tiled=True)]
    squeeze x1 -> x0, local copies, waits for them, and re-layouts: 1.27 us -> none  [on_device(): high = ring(ret[1], 1)]
    dynamic_slice x0 -> x4, local copies, waits for them, and re-layouts: none -> 1.2 us  [the longest x1 0.99 us: on_device(): there_o = lax.dynamic_index_in_dim(w_recv, 1 - chip, axis=1, keepdims=False)]
    dot_general x4, matrix products: 2.13 us -> 3.02 us  [nn(): return jnp.dot(a, b, preferred_element_type=F32)]
  transfers between devices with their start and end apart: 8 -> 8, of which waited for: 5 -> 2; matrix products, arithmetic and copies ran while one was open for 9% -> 10% of each run, Pallas kernels for 17% -> 23%
where the time goes in v3:
time: 73.4 us; the launch traced here: 73 us
  starting transfers between devices  26.4 us (36%)
  Pallas kernels  25.7 us (35%)
  waiting for transfers between devices  8.79 us (12%)
  matrix products  4.77 us (6%)
  local copies, waits for them, and re-layouts  3.6 us (5%)
  other arithmetic  3.02 us (4%)
  between operations  0.76 us (1%)
    pallas_call x4, Pallas kernels, call(): pl.pallas_call(body, out_shape=outs, in_specs=[sm] * scalars + [vm] * (le...  25.7 us
    ppermute x4, starting transfers between devices, ring(): return lax.ppermute(x, 'tm', [(i, (i + by) % n) for i in range(n)])  14.4 us
    all_to_all x1, starting transfers between devices, on_device(): lax.all_to_all(w_mine.reshape(tm_count, -1, width), 'tm', 0, 0, tiled=True)  7.66 us
    ppermute x4, waiting for transfers between devices, ring(): return lax.ppermute(x, 'tm', [(i, (i + by) % n) for i in range(n)])  4.42 us
    ppermute x1, waiting for transfers between devices, chip_swap(): return lax.ppermute(x, 'head', [(0, 2), (2, 0), (1, 3), (3, 1)])  4.36 us
    dot_general x4, matrix products, nn(): return jnp.dot(a, b, preferred_element_type=F32)  3.02 us
    ppermute x1, starting transfers between devices, chip_swap(): return lax.ppermute(x, 'head', [(0, 2), (2, 0), (1, 3), (3, 1)])  2.52 us
    ppermute x2, starting transfers between devices, core_swap(): return lax.ppermute(x, 'head', [(0, 1), (1, 0), (2, 3), (3, 2)])  1.77 us
  transfers between devices with their start and end apart: 8, of which 2 were waited for; matrix products, arithmetic and copies ran while one was open for 10% of the time, Pallas kernels for 23%

profile of v3, /device:TPU:1, one launch (start us, length us, event | category | flops | bytes accessed | tf_op | source)
XLA Modules:
  0.0 73.0 jit_solution(1359356560673645585)
XLA Ops:
  0.6 1.3 %fusion.3 = (bf16[512,256]{1,0:T(8,128)(2,1)S(1)}, bf16[512,256]{1,0:T(8,128)(2,1)S(1)}, bf16[512,256]{1,0:T(8,128)(2,1)S(1)}, bf16[512,256]{1,0:T(8,128)(2,1)S(1)}) fusion(bf16[1024,256]{1,0:T(8,128)(2,1)} %k.5, bf16[1024,256]{1,0:T(8,128)(2,1)} %v.5), kind=kLoop, calls=%fused_computation.15 | loop fusion | bytes 2097152 | tf_op jit(solution)/shard_map/slice | solution.py:315
  1.9 0.8 %pad_maximum_fusion = bf16[1024,256]{1,0:T(8,128)(2,1)} fusion(bf16[512,256]{1,0:T(8,128)(2,1)S(1)} %get-tuple-element.57, bf16[512,256]{1,0:T(8,128)(2,1)S(1)} %get-tuple-element.52), kind=kLoop, calls=%fused_computation.6 | loop fusion | flops 1048576 | bytes 1048576 | tf_op jit(solution)/shard_map/concatenate | solution.py:314
  2.7 2.1 %collective-permute-start = (bf16[1024,256]{1,0:T(8,128)(2,1)}, bf16[1024,256]{1,0:T(8,128)(2,1)}, u32[]{:S(2)}, u32[]{:S(2)}) collective-permute-start(bf16[1024,256]{1,0:T(8,128)(2,1)} %pad_maximum_fusion), channel_id=1, source_target_pairs={{0,4},{4,8},{8,12},{12,16},{16,20},{20,24},{24,28},{28,32},{32,36}... | collective-permute-start | bytes 1572872 | tf_op jit(solution)/shard_map/ppermute | solution.py:16
  4.8 0.8 %pad_maximum_fusion.1 = bf16[1024,256]{1,0:T(8,128)(2,1)} fusion(bf16[512,256]{1,0:T(8,128)(2,1)S(1)} %get-tuple-element.58, bf16[512,256]{1,0:T(8,128)(2,1)S(1)} %get-tuple-element.51), kind=kLoop, calls=%fused_computation.7 | loop fusion | flops 1048576 | bytes 1048576 | tf_op jit(solution)/shard_map/concatenate | solution.py:315
  5.7 0.0 copy-start.1
  5.7 5.8 %collective-permute-start.1 = (bf16[1024,256]{1,0:T(8,128)(2,1)}, bf16[1024,256]{1,0:T(8,128)(2,1)}, u32[]{:S(2)}, u32[]{:S(2)}) collective-permute-start(bf16[1024,256]{1,0:T(8,128)(2,1)} %pad_maximum_fusion.1), channel_id=1, source_target_pairs={{0,124},{4,0},{8,4},{12,8},{16,12},{20,16},{24,20},{28,24},{32,28}... | collective-permute-start | bytes 1572872 | tf_op jit(solution)/shard_map/ppermute | solution.py:16
  11.5 0.7 pad_add_fusion.where
  12.2 5.9 %shard_map.101 = (bf16[2,2,512,1024]{3,2,1,0:T(8,128)(2,1)}, f32[8,2,512]{2,1,0:T(2,128)}, f32[256,1024]{1,0:T(8,128)}) custom-call(s32[2]{0:T(128)} %pad_add_fusion.where, s32[8,5]{1,0:T(8,128)} %lists.3, bf16[1024,256]{1,0:T(8,128)(2,1)} %q.5, bf16[1024,256]{1,0:T(8,128)(2,1)} %k.5, bf16[1024,256]{1,0:T(8,128)(2,1)} %v.5), custom_call_target="tpu_custom_call" | custom-call | flops 1000000000 | bytes 8388608 | tf_op jit(solution)/shard_map/pallas_call | solution.py:286
  18.1 0.0 copy-start
  18.1 0.0 copy-done.1
  18.1 0.2 copy.14
  18.3 0.7 constant_dynamic-slice_fusion.3
  19.0 1.0 %collective-permute-start.2 = (bf16[256,512]{0,1:T(8,128)(2,1)}, bf16[256,512]{0,1:T(8,128)(2,1)}, u32[]{:S(2)}, u32[]{:S(2)}) collective-permute-start(bf16[256,512]{0,1:T(8,128)(2,1)} %bitcast.3), channel_id=1, source_target_pairs={{0,1},{1,0},{2,3},{3,2},{4,5},{5,4},{6,7},{7,6},{8,9},{9,8},{10,11... | collective-permute-start | bytes 786440 | tf_op jit(solution)/shard_map/ppermute | solution.py:20
  20.0 0.1 copy.17
  20.1 0.1 copy.15
  20.2 0.0 copy-done
  20.2 1.7 %fusion.5.ga = f32[256,1024]{1,0:T(8,128)} fusion(bf16[256,1024]{1,0:T(8,128)(2,1)S(1)} %copy-done.1, bf16[1024,1024]{1,0:T(8,128)(2,1)S(1)} %copy-done), kind=kOutput, calls=%fused_computation.17 | convolution fusion | flops 536870912 | bytes 3670016 | tf_op jit(solution)/shard_map/dot_general | solution.py:317
  22.0 0.0 collective-permute-done.2
  22.0 1.0 %constant_dynamic-slice_fusion = (bf16[256,1,256]{0,2,1:T(8,128)(2,1)S(1)}, bf16[256,1,256]{0,2,1:T(8,128)(2,1)S(1)}) fusion(bf16[256,2,256]{0,2,1:T(8,128)(2,1)} %bitcast.4, s32[]{:T(128)S(6)} %select_n.40, s32[]{:T(128)S(6)} %select_n.34), kind=kLoop, calls=%fused_computation.9 | loop fusion | bytes 524296 | tf_op jit(solution)/shard_map/jit(dynamic_index_in_dim)/dynamic_slice | solution.py:339
  22.9 0.1 copy.20
  23.1 0.1 copy.19
  23.2 0.0 collective-permute-done.kvu
  23.2 0.0 collective-permute-done.1.kvd
  23.2 9.0 %shard_map.102 = (bf16[1024,256]{1,0:T(8,128)(2,1)}, bf16[256,1024]{1,0:T(8,128)(2,1)}, bf16[1024,256]{1,0:T(8,128)(2,1)}, f32[8,1,512]{2,1,0:T(1,128)}, bf16[10...) custom-call(s32[2]{0:T(128)} %pad_add_fusion.where, s32[8,5]{1,0:T(8,128)} %lists.3, ...), custom_call_target="tpu_custom_call" | custom-call | flops 4000000000 | bytes 8388608 | tf_op jit(solution)/shard_map/pallas_call | solution.py:286
  32.2 0.8 %collective-permute-start.3 = (bf16[1024,256]{1,0:T(8,128)(2,1)}, bf16[1024,256]{1,0:T(8,128)(2,1)S(1)}, u32[]{:S(2)}, u32[]{:S(2)}) collective-permute-start(bf16[1024,256]{1,0:T(8,128)(2,1)} %get-tuple-element.32), channel_id=1, source_target_pairs={{0,1},{1,0},{2,3},{3,2},{4,5},{5,4},{6,7},{7,6},{8,9},{9,8},{10,11... | collective-permute-start | bytes 1572872 | tf_op jit(solution)/shard_map/ppermute | solution.py:20
  33.0 6.4 %collective-permute-start.5 = (bf16[1024,256]{1,0:T(8,128)(2,1)}, bf16[1024,256]{1,0:T(8,128)(2,1)S(1)}, u32[]{:S(2)}, u32[]{:S(2)}) collective-permute-start(bf16[1024,256]{1,0:T(8,128)(2,1)} %get-tuple-element.44), channel_id=1, source_target_pairs={{0,124},{4,0},{8,4},{12,8},{16,12},{20,16},{24,20},{28,24},{32,28}... | collective-permute-start | bytes 1572872 | tf_op jit(solution)/shard_map/ppermute | solution.py:16
  39.4 0.0 collective-permute-start.6
  39.4 0.0 collective-permute-done.3
  39.4 3.4 %shard_map.104 = bf16[1024,256]{1,0:T(8,128)(2,1)} custom-call(bf16[256,1024]{1,0:T(8,128)(2,1)} %get-tuple-element.48.at, bf16[1024,1024]{1,0:T(8,128)(2,1)} %go.1), custom_call_target="tpu_custom_call" | custom-call | flops 1000000000 | bytes 8388608 | tf_op jit(solution)/shard_map/pallas_call | solution.py:286
  42.8 0.0 copy-start.2
  42.8 7.7 %all-to-all-start = ((bf16[32,32,256]{2,1,0:T(8,128)(2,1)}), bf16[32,32,256]{2,1,0:T(8,128)(2,1)S(1)}, u32[]{:S(2)}, u32[]{:S(2)}) async-start(bf16[32,32,256]{2,1,0:T(8,128)(2,1)} %bitcast.24), calls=%async_computation | async-start | bytes 1048576 | tf_op jit(solution)/shard_map/all_to_all | solution.py:378
  50.5 0.3 fusion.7
  50.8 0.0 copy-done.2
  50.8 0.3 fusion.2
  51.1 2.5 %collective-permute-start.4 = (bf16[1024,256]{1,0:T(8,128)(2,1)S(1)}, bf16[1024,256]{1,0:T(8,128)(2,1)}, u32[]{:S(2)}, u32[]{:S(2)}) collective-permute-start(bf16[1024,256]{1,0:T(8,128)(2,1)S(1)} %fusion.2), channel_id=1, source_target_pairs={{0,2},{2,0},{1,3},{3,1},{4,6},{6,4},{5,7},{7,5},{8,10},{10,8},{9,1... | collective-permute-start | bytes 1572872 | tf_op jit(solution)/shard_map/ppermute | solution.py:24
  53.6 0.0 collective-permute-done.5.low
  53.6 0.0 copy-start.3
  53.6 4.4 %collective-permute-done.6.high = bf16[1024,256]{1,0:T(8,128)(2,1)} collective-permute-done((bf16[1024,256]{1,0:T(8,128)(2,1)}, bf16[1024,256]{1,0:T(8,128)(2,1)}, u32[]{:S(2)}, u32[]{:S(2)}) %collective-permute-start.6) | collective-permute-done | bytes 524320 | tf_op jit(solution)/shard_map/ppermute | solution.py:16
  58.0 0.0 copy-done.3
  58.0 7.4 %shard_map.103 = (bf16[1024,256]{1,0:T(8,128)(2,1)}, bf16[1024,256]{1,0:T(8,128)(2,1)}, bf16[1024,256]{1,0:T(8,128)(2,1)}) custom-call(s32[2]{0:T(128)} %pad_add_fusion.where, bf16[1024,256]{1,0:T(8,128)(2,1)} %q.5, bf16[1024,256]{1,0:T(8,128)(2,1)} %k.5, bf16[1024,256]{1,0:T(8,128)(2,1)} %v.5, bf16[2,2,512,1024]{3,2,1,0:T(8,128)(2,1)} %get-tuple-element.39.p, ...), custom_call_target="tpu_custom_call" | custom-call | flops 4000000000 | bytes 8388608 | tf_op jit(solution)/shard_map/pallas_call | solution.py:286
  65.5 0.3 fusion.6
  65.8 0.0 all-to-all-done
  65.8 0.1 convert_reduce_fusion
  65.9 0.6 multiply_bitcast_fusion
  66.5 4.4 %collective-permute-done.4 = bf16[1024,256]{1,0:T(8,128)(2,1)} collective-permute-done((bf16[1024,256]{1,0:T(8,128)(2,1)S(1)}, bf16[1024,256]{1,0:T(8,128)(2,1)}, u32[]{:S(2)}, u32[]{:S(2)}) %collective-permute-start.4) | collective-permute-done | bytes 524320 | tf_op jit(solution)/shard_map/ppermute | solution.py:24
  70.9 2.1 %fusion.1 = bf16[1024,256]{1,0:T(8,128)(2,1)} fusion(f32[1024,256]{1,0:T(8,128)S(1)} %fusion.6, bf16[1024,256]{1,0:T(8,128)(2,1)S(1)} %copy-done.2, bf16[256,256]{1,0:T(8,128)(2,1)S(1)} %bitcast.27, bf16[1024,256]{1,0:T(8,128)(2,1)} %collective-permute-done.4), kind=kOutput, calls=%fused_computation.3 | convolution fusion | flops 135266304 | bytes 2752512 | tf_op jit(solution)/shard_map/dot_general | solution.py:32
  (1 shorter events, 0.0 us)
Async XLA Ops:
  2.7 20.4 %collective-permute-start = (bf16[1024,256]{1,0:T(8,128)(2,1)}, bf16[1024,256]{1,0:T(8,128)(2,1)}, u32[]{:S(2)}, u32[]{:S(2)}) collective-permute-start(bf16[1024,256]{1,0:T(8,128)(2,1)} %pad_maximum_fusion), channel_id=1, source_target_pairs={{0,4},{4,8},{8,12},{12,16},{16,20},{20,24},{24,28},{28,32},{32,36}... | collective-permute-start | bytes 1572872 | tf_op jit(solution)/shard_map/ppermute | solution.py:16
  5.7 12.4 %copy-start.1 = (bf16[256,1024]{1,0:T(8,128)(2,1)S(1)}, bf16[256,1024]{1,0:T(8,128)(2,1)}, u32[]{:S(2)}) copy-start(bf16[256,1024]{1,0:T(8,128)(2,1)} %param.9) | copy-start | bytes 1572868
  5.7 17.5 %collective-permute-start.1 = (bf16[1024,256]{1,0:T(8,128)(2,1)}, bf16[1024,256]{1,0:T(8,128)(2,1)}, u32[]{:S(2)}, u32[]{:S(2)}) collective-permute-start(bf16[1024,256]{1,0:T(8,128)(2,1)} %pad_maximum_fusion.1), channel_id=1, source_target_pairs={{0,124},{4,0},{8,4},{12,8},{16,12},{20,16},{24,20},{28,24},{32,28}... | collective-permute-start | bytes 1572872 | tf_op jit(solution)/shard_map/ppermute | solution.py:16
  18.1 2.1 %copy-start = (bf16[1024,1024]{1,0:T(8,128)(2,1)S(1)}, bf16[1024,1024]{1,0:T(8,128)(2,1)}, u32[]{:S(2)}) copy-start(bf16[1024,1024]{1,0:T(8,128)(2,1)} %go.1) | copy-start | bytes 6291460
  19.0 3.0 %collective-permute-start.2 = (bf16[256,512]{0,1:T(8,128)(2,1)}, bf16[256,512]{0,1:T(8,128)(2,1)}, u32[]{:S(2)}, u32[]{:S(2)}) collective-permute-start(bf16[256,512]{0,1:T(8,128)(2,1)} %bitcast.3), channel_id=1, source_target_pairs={{0,1},{1,0},{2,3},{3,2},{4,5},{5,4},{6,7},{7,6},{8,9},{9,8},{10,11... | collective-permute-start | bytes 786440 | tf_op jit(solution)/shard_map/ppermute | solution.py:20
  32.2 7.3 %collective-permute-start.3 = (bf16[1024,256]{1,0:T(8,128)(2,1)}, bf16[1024,256]{1,0:T(8,128)(2,1)S(1)}, u32[]{:S(2)}, u32[]{:S(2)}) collective-permute-start(bf16[1024,256]{1,0:T(8,128)(2,1)} %get-tuple-element.32), channel_id=1, source_target_pairs={{0,1},{1,0},{2,3},{3,2},{4,5},{5,4},{6,7},{7,6},{8,9},{9,8},{10,11... | collective-permute-start | bytes 1572872 | tf_op jit(solution)/shard_map/ppermute | solution.py:20
  33.0 20.6 %collective-permute-start.5 = (bf16[1024,256]{1,0:T(8,128)(2,1)}, bf16[1024,256]{1,0:T(8,128)(2,1)S(1)}, u32[]{:S(2)}, u32[]{:S(2)}) collective-permute-start(bf16[1024,256]{1,0:T(8,128)(2,1)} %get-tuple-element.44), channel_id=1, source_target_pairs={{0,124},{4,0},{8,4},{12,8},{16,12},{20,16},{24,20},{28,24},{32,28}... | collective-permute-start | bytes 1572872 | tf_op jit(solution)/shard_map/ppermute | solution.py:16
  39.4 18.6 %collective-permute-start.6 = (bf16[1024,256]{1,0:T(8,128)(2,1)}, bf16[1024,256]{1,0:T(8,128)(2,1)}, u32[]{:S(2)}, u32[]{:S(2)}) collective-permute-start(bf16[1024,256]{1,0:T(8,128)(2,1)} %get-tuple-element.43.ret), channel_id=1, source_target_pairs={{0,4},{4,8},{8,12},{12,16},{16,20},{20,24},{24,28},{28,32},{32,36}... | collective-permute-start | bytes 1572872 | tf_op jit(solution)/shard_map/ppermute | solution.py:16
  42.8 8.0 %copy-start.2 = (bf16[1024,256]{1,0:T(8,128)(2,1)S(1)}, bf16[1024,256]{1,0:T(8,128)(2,1)}, u32[]{:S(2)}) copy-start(bf16[1024,256]{1,0:T(8,128)(2,1)} %get-tuple-element.32) | copy-start | bytes 1572868
  42.8 23.0 %all-to-all-start = ((bf16[32,32,256]{2,1,0:T(8,128)(2,1)}), bf16[32,32,256]{2,1,0:T(8,128)(2,1)S(1)}, u32[]{:S(2)}, u32[]{:S(2)}) async-start(bf16[32,32,256]{2,1,0:T(8,128)(2,1)} %bitcast.24), calls=%async_computation | async-start | bytes 1048576 | tf_op jit(solution)/shard_map/all_to_all | solution.py:378
  51.1 19.8 %collective-permute-start.4 = (bf16[1024,256]{1,0:T(8,128)(2,1)S(1)}, bf16[1024,256]{1,0:T(8,128)(2,1)}, u32[]{:S(2)}, u32[]{:S(2)}) collective-permute-start(bf16[1024,256]{1,0:T(8,128)(2,1)S(1)} %fusion.2), channel_id=1, source_target_pairs={{0,2},{2,0},{1,3},{3,1},{4,6},{6,4},{5,7},{7,5},{8,10},{10,8},{9,1... | collective-permute-start | bytes 1572872 | tf_op jit(solution)/shard_map/ppermute | solution.py:24
  53.6 4.4 %copy-start.3 = (bf16[1024,256]{1,0:T(8,128)(2,1)}, bf16[1024,256]{1,0:T(8,128)(2,1)S(1)}, u32[]{:S(2)}) copy-start(bf16[1024,256]{1,0:T(8,128)(2,1)S(1)} %collective-permute-done.5.low) | copy-start | bytes 1572868

commit v4 on v3

--- a/solution.py
+++ b/solution.py
@@ -81,7 +81,7 @@
 
 
 def first_tile(where, half, n_tile):
-    return (where[0] if half == 0 else 2 * where[1] - 1 - where[0]) * n_tile
+    return (where[0] if half == 0 else 2 * lax.axis_size("tm") - 1 - where[0]) * n_tile
 
 
 def staged(items, stages):
@@ -148,7 +148,7 @@
     pairs = q.shape[1] // (2 * HD)
     span = k.shape[0] // 2
     n_tile = span // T
-    is_last = where[0] == where[1] - 1
+    is_last = where[0] == lax.axis_size("tm") - 1
     for half in range(2):
         if half == 0:
             kp[half] = kvu[:span]
@@ -230,7 +230,7 @@
     pairs = q.shape[1] // (2 * HD)
     span = k.shape[0] // 2
     n_tile = span // T
-    is_last = where[0] == where[1] - 1
+    is_last = where[0] == lax.axis_size("tm") - 1
     is_first = where[0] == 0
     kt[...] = k[...].T
 
@@ -303,7 +303,7 @@
     tm_count = lax.axis_size("tm")
     tm_index = lax.axis_index("tm")
     head_index = lax.axis_index("head")
-    where = jnp.stack([tm_index, jnp.int32(tm_count)]).astype(jnp.int32)
+    where = tm_index.astype(jnp.int32).reshape(1)
 
     def arr(dtype, *dims):
         return jax.ShapeDtypeStruct(dims, dtype)
@@ -313,6 +313,13 @@
 
     kvu = ring(jnp.concatenate([keys[:span], values[:span]], axis=0), 1)
     kvd = ring(jnp.concatenate([keys[span:], values[span:]], axis=0), -1)
+
+    w4 = out_weight.reshape(width, 2, 2, width)
+    core = head_index % 2
+    chip = head_index // 2
+    w_core = lax.dynamic_index_in_dim(w4, core, axis=2, keepdims=False)
+    w_send = lax.dynamic_index_in_dim(w4, 1 - core, axis=2, keepdims=False)
+    w_recv = core_swap(w_send.reshape(width, 2 * width)).reshape(width, 2, width)
 
     ga = lax.dot_general(out_weight, grad_output, (((1,), (1,)), ((), ())), preferred_element_type=F32)
 
@@ -328,18 +335,6 @@
         keys,
         values,
     )
-    st, weight = lax.optimization_barrier((st, out_weight))
-    w4 = weight.reshape(width, 2, 2, width)
-    core = head_index % 2
-    chip = head_index // 2
-    w_core = lax.dynamic_index_in_dim(w4, core, axis=2, keepdims=False)
-    w_send = lax.dynamic_index_in_dim(w4, 1 - core, axis=2, keepdims=False)
-    w_recv = core_swap(w_send.reshape(width, 2 * width)).reshape(width, 2, width)
-    there = lax.dynamic_index_in_dim(w_core, 1 - chip, axis=1, keepdims=False)
-    there_o = lax.dynamic_index_in_dim(w_recv, 1 - chip, axis=1, keepdims=False)
-    here = lax.dynamic_index_in_dim(w_core, chip, axis=1, keepdims=False)
-    here_o = lax.dynamic_index_in_dim(w_recv, chip, axis=1, keepdims=False)
-    st, here, here_o, there, there_o = lax.optimization_barrier((st, here, here_o, there, there_o))
     att, at, g, dl, ret_low, ret_high, dqp = call(
         halo_kernel,
         [
@@ -374,6 +369,10 @@
     att_other = core_swap(att)
     at, att_other = lax.optimization_barrier((at, att_other))
     (w_mine,) = call(weight_kernel, [arr(BF16, grad_output.shape[1], width)], [], 0, 10**9, at, grad_output)
+    there = lax.dynamic_index_in_dim(w_core, 1 - chip, axis=1, keepdims=False)
+    there_o = lax.dynamic_index_in_dim(w_recv, 1 - chip, axis=1, keepdims=False)
+    here = lax.dynamic_index_in_dim(w_core, chip, axis=1, keepdims=False)
+    here_o = lax.dynamic_index_in_dim(w_recv, chip, axis=1, keepdims=False)
     out_recv = chip_swap((nn(att, there) + nn(att_other, there_o)).astype(BF16))
     w_parts = lax.all_to_all(w_mine.reshape(tm_count, -1, width), "tm", 0, 0, tiled=True)
 

time: 73.4 us -> 76.2 us (1.038)
  waiting for transfers between devices: 8.79 us -> 16.7 us
  starting transfers between devices: 26.4 us -> 22.3 us
  other arithmetic: 3.02 us -> 1.57 us
  local copies, waits for them, and re-layouts: 3.6 us -> 2.48 us
  matrix products: 4.77 us -> 5.74 us
    all_to_all x1, waiting for transfers between devices: 0.01 us -> 7.06 us  [on_device(): lax.all_to_all(w_mine.reshape(tm_count, -1, width), 'tm', 0, 0, tiled=True)]
    ppermute x4, waiting for transfers between devices: 4.42 us -> 9.68 us  [ring(): return lax.ppermute(x, 'tm', [(i, (i + by) % n) for i in range(n)])]
    ppermute x1, waiting for transfers between devices: 4.36 us -> 0.01 us  [chip_swap(): return lax.ppermute(x, 'head', [(0, 2), (2, 0), (1, 3), (3, 1)])]
    all_to_all x1, starting transfers between devices: 7.66 us -> 4.07 us  [on_device(): lax.all_to_all(w_mine.reshape(tm_count, -1, width), 'tm', 0, 0, tiled=True)]
    dynamic_slice x4 -> x0, local copies, waits for them, and re-layouts: 1.2 us -> none  [the longest x1 0.99 us: on_device(): there_o = lax.dynamic_index_in_dim(w_recv, 1 - chip, axis=1, keepdims=False)]
    unnamed x10 -> x11, local copies, waits for them, and re-layouts: 0.21 us -> 1.19 us
    dot_general x4, matrix products: 3.02 us -> 4 us  [nn(): return jnp.dot(a, b, preferred_element_type=F32)]
    concatenate x1, other arithmetic: 0.83 us -> 0.04 us  [on_device(): kvd = ring(jnp.concatenate([keys[span:], values[span:]], axis=0), -1)]
  transfers between devices with their start and end apart: 8 -> 8, of which waited for: 2 -> 4; matrix products, arithmetic and copies ran while one was open for 10% -> 7% of each run, Pallas kernels for 23% -> 22%
where the time goes in v4:
time: 76.2 us; the launch traced here: 75.4 us
  Pallas kernels  25.8 us (34%)
  starting transfers between devices  22.3 us (29%)
  waiting for transfers between devices  16.7 us (22%)
  matrix products  5.74 us (8%)
  local copies, waits for them, and re-layouts  2.48 us (3%)
  other arithmetic  1.57 us (2%)
    pallas_call x4, Pallas kernels, call(): pl.pallas_call(body, out_shape=outs, in_specs=[sm] * scalars + [vm] * (le...  25.8 us
    ppermute x4, starting transfers between devices, ring(): return lax.ppermute(x, 'tm', [(i, (i + by) % n) for i in range(n)])  13.8 us
    ppermute x4, waiting for transfers between devices, ring(): return lax.ppermute(x, 'tm', [(i, (i + by) % n) for i in range(n)])  9.68 us
    all_to_all x1, waiting for transfers between devices, on_device(): lax.all_to_all(w_mine.reshape(tm_count, -1, width), 'tm', 0, 0, tiled=True)  7.06 us
    all_to_all x1, starting transfers between devices, on_device(): lax.all_to_all(w_mine.reshape(tm_count, -1, width), 'tm', 0, 0, tiled=True)  4.07 us
    dot_general x4, matrix products, nn(): return jnp.dot(a, b, preferred_element_type=F32)  4 us
    ppermute x1, starting transfers between devices, chip_swap(): return lax.ppermute(x, 'head', [(0, 2), (2, 0), (1, 3), (3, 1)])  2.45 us
    ppermute x2, starting transfers between devices, core_swap(): return lax.ppermute(x, 'head', [(0, 1), (1, 0), (2, 3), (3, 2)])  2.04 us
  transfers between devices with their start and end apart: 8, of which 4 were waited for; matrix products, arithmetic and copies ran while one was open for 7% of the time, Pallas kernels for 22%

profile of v4, /device:TPU:1, one launch (start us, length us, event | category | flops | bytes accessed | tf_op | source)
XLA Modules:
  0.0 75.4 jit_solution(18024603123242942825)
XLA Ops:
  0.6 1.3 %fusion.17 = (bf16[512,256]{1,0:T(8,128)(2,1)S(1)}, bf16[512,256]{1,0:T(8,128)(2,1)S(1)}, bf16[512,256]{1,0:T(8,128)(2,1)S(1)}, bf16[512,256]{1,0:T(8,128)(2,1)S(1)}) fusion(bf16[1024,256]{1,0:T(8,128)(2,1)} %k.5, bf16[1024,256]{1,0:T(8,128)(2,1)} %v.5), kind=kLoop, calls=%fused_computation.24 | loop fusion | bytes 2097152 | tf_op jit(solution)/shard_map/slice | solution.py:315
  1.9 8.0 %collective-permute-start.1 = (bf16[1024,256]{1,0:T(8,128)(2,1)S(1)}, bf16[1024,256]{1,0:T(8,128)(2,1)}, u32[]{:S(2)}, u32[]{:S(2)}) collective-permute-start(bf16[1024,256]{1,0:T(8,128)(2,1)S(1)} %pad_maximum_fusion.1), channel_id=1, source_target_pairs={{0,124},{4,0},{8,4},{12,8},{16,12},{20,16},{24,20},{28,24},{32,28}... | collective-permute-start | bytes 1572872 | tf_op jit(solution)/shard_map/ppermute | solution.py:16
  10.0 0.8 %pad_maximum_fusion = bf16[1024,256]{1,0:T(8,128)(2,1)} fusion(bf16[512,256]{1,0:T(8,128)(2,1)S(1)} %get-tuple-element.39, bf16[512,256]{1,0:T(8,128)(2,1)S(1)} %get-tuple-element.36), kind=kLoop, calls=%fused_computation.6 | loop fusion | flops 1048576 | bytes 1048576 | tf_op jit(solution)/shard_map/concatenate | solution.py:314
  10.8 0.0 copy-start
  10.8 0.0 copy-start.1
  10.8 0.0 collective-permute-start
  10.8 6.0 %shard_map.101 = (bf16[2,2,512,1024]{3,2,1,0:T(8,128)(2,1)}, f32[8,2,512]{2,1,0:T(2,128)}, f32[256,1024]{1,0:T(8,128)}) custom-call(s32[1]{0:T(128)} %bitcast.where, s32[8,5]{1,0:T(8,128)} %lists.3, bf16[1024,256]{1,0:T(8,128)(2,1)} %q.5, bf16[1024,256]{1,0:T(8,128)(2,1)} %k.5, bf16[1024,256]{1,0:T(8,128)(2,1)} %v.5), custom_call_target="tpu_custom_call" | custom-call | flops 1000000000 | bytes 8388608 | tf_op jit(solution)/shard_map/pallas_call | solution.py:286
  16.8 0.0 copy-done
  16.8 0.0 copy-done.1
  16.8 1.7 %fusion.19.ga = f32[256,1024]{1,0:T(8,128)} fusion(bf16[256,1024]{1,0:T(8,128)(2,1)S(1)} %copy-done.1, bf16[1024,1024]{1,0:T(8,128)(2,1)S(1)} %copy-done), kind=kOutput, calls=%fused_computation.26 | convolution fusion | flops 536870912 | bytes 3670016 | tf_op jit(solution)/shard_map/dot_general | solution.py:324
  18.6 2.0 %collective-permute-done.1.kvd = bf16[1024,256]{1,0:T(8,128)(2,1)} collective-permute-done((bf16[1024,256]{1,0:T(8,128)(2,1)S(1)}, bf16[1024,256]{1,0:T(8,128)(2,1)}, u32[]{:S(2)}, u32[]{:S(2)}) %collective-permute-start.1) | collective-permute-done | bytes 524320 | tf_op jit(solution)/shard_map/ppermute | solution.py:16
  20.6 7.2 %collective-permute-done.kvu = bf16[1024,256]{1,0:T(8,128)(2,1)} collective-permute-done((bf16[1024,256]{1,0:T(8,128)(2,1)}, bf16[1024,256]{1,0:T(8,128)(2,1)}, u32[]{:S(2)}, u32[]{:S(2)}) %collective-permute-start) | collective-permute-done | bytes 524320 | tf_op jit(solution)/shard_map/ppermute | solution.py:16
  27.8 9.0 %shard_map.102 = (bf16[1024,256]{1,0:T(8,128)(2,1)}, bf16[256,1024]{1,0:T(8,128)(2,1)}, bf16[1024,256]{1,0:T(8,128)(2,1)}, f32[8,1,512]{2,1,0:T(1,128)}, bf16[10...) custom-call(s32[1]{0:T(128)} %bitcast.where, s32[8,5]{1,0:T(8,128)} %lists.3, ...), custom_call_target="tpu_custom_call" | custom-call | flops 4000000000 | bytes 8388608 | tf_op jit(solution)/shard_map/pallas_call | solution.py:286
  36.8 0.0 copy-start.2
  36.8 1.9 %collective-permute-start.2 = (bf16[1024,256]{1,0:T(8,128)(2,1)}, bf16[1024,256]{1,0:T(8,128)(2,1)S(1)}, u32[]{:S(2)}, u32[]{:S(2)}) collective-permute-start(bf16[1024,256]{1,0:T(8,128)(2,1)} %get-tuple-element.22), channel_id=1, source_target_pairs={{0,1},{1,0},{2,3},{3,2},{4,5},{5,4},{6,7},{7,6},{8,9},{9,8},{10,11... | collective-permute-start | bytes 1572872 | tf_op jit(solution)/shard_map/ppermute | solution.py:20
  38.8 0.2 copy.14
  39.0 0.1 collective-permute-start.3
  39.2 0.1 collective-permute-start.6
  39.2 5.7 %collective-permute-start.5 = (bf16[1024,256]{1,0:T(8,128)(2,1)}, bf16[1024,256]{1,0:T(8,128)(2,1)S(1)}, u32[]{:S(2)}, u32[]{:S(2)}) collective-permute-start(bf16[1024,256]{1,0:T(8,128)(2,1)} %get-tuple-element.30), channel_id=1, source_target_pairs={{0,124},{4,0},{8,4},{12,8},{16,12},{20,16},{24,20},{28,24},{32,28}... | collective-permute-start | bytes 1572872 | tf_op jit(solution)/shard_map/ppermute | solution.py:16
  44.9 0.0 collective-permute-done.2
  44.9 0.0 collective-permute-done.3
  44.9 0.3 fusion.3
  45.2 0.0 copy-done.2
  45.3 1.2 %fusion.2 = bf16[1024,256]{1,0:T(8,128)(2,1)} fusion(f32[1024,256]{1,0:T(8,128)S(1)} %fusion.3, bf16[1024,256]{1,0:T(8,128)(2,1)S(1)} %copy-done.2, bf16[256,2,2,256]{0,3,2,1:T(8,128)(2,1)S(1)} %bitcast.30, s32[]{:T(128)S(6)} %select_n.41, s32[]{:T(128)S(6)} %select_n.38), kind=kOutput, calls=%fused_computation.4 | convolution fusion | flops 134742016 | bytes 2228232 | tf_op jit(solution)/shard_map/dot_general | solution.py:32
  46.4 2.5 %collective-permute-start.4 = (bf16[1024,256]{1,0:T(8,128)(2,1)}, bf16[1024,256]{1,0:T(8,128)(2,1)}, u32[]{:S(2)}, u32[]{:S(2)}) collective-permute-start(bf16[1024,256]{1,0:T(8,128)(2,1)} %fusion.2), channel_id=1, source_target_pairs={{0,2},{2,0},{1,3},{3,1},{4,6},{6,4},{5,7},{7,5},{8,10},{10,8},{9,1... | collective-permute-start | bytes 1572872 | tf_op jit(solution)/shard_map/ppermute | solution.py:24
  48.9 3.4 %shard_map.104 = bf16[1024,256]{1,0:T(8,128)(2,1)} custom-call(bf16[256,1024]{1,0:T(8,128)(2,1)} %get-tuple-element.34.at, bf16[1024,1024]{1,0:T(8,128)(2,1)} %go.1), custom_call_target="tpu_custom_call" | custom-call | flops 1000000000 | bytes 8388608 | tf_op jit(solution)/shard_map/pallas_call | solution.py:286
  52.2 4.1 %all-to-all-start = ((bf16[32,32,256]{2,1,0:T(8,128)(2,1)}), bf16[32,32,256]{2,1,0:T(8,128)(2,1)S(1)}, u32[]{:S(2)}, u32[]{:S(2)}) async-start(bf16[32,32,256]{2,1,0:T(8,128)(2,1)} %bitcast.32), calls=%async_computation | async-start | bytes 1048576 | tf_op jit(solution)/shard_map/all_to_all | solution.py:377
  56.3 0.5 collective-permute-done.6.high
  56.8 0.0 copy-start.3
  56.8 0.0 collective-permute-done.5.low
  56.8 0.0 copy-start.4
  56.8 0.8 %copy-done.3 = bf16[1024,256]{1,0:T(8,128)(2,1)} copy-done((bf16[1024,256]{1,0:T(8,128)(2,1)}, bf16[1024,256]{1,0:T(8,128)(2,1)S(1)}, u32[]{:S(2)}) %copy-start.3) | copy-done | bytes 524312
  57.6 0.1 copy-done.4
  57.8 7.4 %shard_map.103 = (bf16[1024,256]{1,0:T(8,128)(2,1)}, bf16[1024,256]{1,0:T(8,128)(2,1)}, bf16[1024,256]{1,0:T(8,128)(2,1)}) custom-call(s32[1]{0:T(128)} %bitcast.where, bf16[1024,256]{1,0:T(8,128)(2,1)} %q.5, bf16[1024,256]{1,0:T(8,128)(2,1)} %k.5, bf16[1024,256]{1,0:T(8,128)(2,1)} %v.5, bf16[2,2,512,1024]{3,2,1,0:T(8,128)(2,1)} %get-tuple-element.25.p, ...), custom_call_target="tpu_custom_call" | custom-call | flops 4000000000 | bytes 8388608 | tf_op jit(solution)/shard_map/pallas_call | solution.py:286
  65.2 0.3 fusion.6
  65.5 7.1 %all-to-all-done = bf16[32,32,256]{2,1,0:T(8,128)(2,1)S(1)} async-done(((bf16[32,32,256]{2,1,0:T(8,128)(2,1)}), bf16[32,32,256]{2,1,0:T(8,128)(2,1)S(1)}, u32[]{:S(2)}, u32[]{:S(2)}) %all-to-all-start) | async-done | bytes 524320 | tf_op jit(solution)/shard_map/all_to_all | solution.py:377
  72.6 0.1 convert_reduce_fusion
  72.7 0.6 multiply_bitcast_fusion
  73.3 0.0 collective-permute-done.4
  73.3 2.2 %fusion.1 = bf16[1024,256]{1,0:T(8,128)(2,1)} fusion(f32[1024,256]{1,0:T(8,128)S(1)} %fusion.6, bf16[1024,256]{1,0:T(8,128)(2,1)S(1)} %copy-done.2, bf16[1024,256]{1,0:T(8,128)(2,1)} %collective-permute-done.4, bf16[256,2,2,256]{0,3,2,1:T(8,128)(2,1)S(1)} %bitcast.31, s32[]{:T(128)S(6)} %select_n.35, s32[]{:T(128)S(6)} %select_n.38), kind=kOutput, calls=%fused_computation.3 | convolution fusion | flops 135266304 | bytes 2752520 | tf_op jit(solution)/shard_map/dot_general | solution.py:32
  (2 shorter events, 0.1 us)
Async XLA Ops:
  1.9 18.6 %collective-permute-start.1 = (bf16[1024,256]{1,0:T(8,128)(2,1)S(1)}, bf16[1024,256]{1,0:T(8,128)(2,1)}, u32[]{:S(2)}, u32[]{:S(2)}) collective-permute-start(bf16[1024,256]{1,0:T(8,128)(2,1)S(1)} %pad_maximum_fusion.1), channel_id=1, source_target_pairs={{0,124},{4,0},{8,4},{12,8},{16,12},{20,16},{24,20},{28,24},{32,28}... | collective-permute-start | bytes 1572872 | tf_op jit(solution)/shard_map/ppermute | solution.py:16
  10.8 6.0 %copy-start = (bf16[1024,1024]{1,0:T(8,128)(2,1)S(1)}, bf16[1024,1024]{1,0:T(8,128)(2,1)}, u32[]{:S(2)}) copy-start(bf16[1024,1024]{1,0:T(8,128)(2,1)} %go.1) | copy-start | bytes 6291460
  10.8 6.0 %copy-start.1 = (bf16[256,1024]{1,0:T(8,128)(2,1)S(1)}, bf16[256,1024]{1,0:T(8,128)(2,1)}, u32[]{:S(2)}) copy-start(bf16[256,1024]{1,0:T(8,128)(2,1)} %param.9) | copy-start | bytes 1572868
  10.8 17.0 %collective-permute-start = (bf16[1024,256]{1,0:T(8,128)(2,1)}, bf16[1024,256]{1,0:T(8,128)(2,1)}, u32[]{:S(2)}, u32[]{:S(2)}) collective-permute-start(bf16[1024,256]{1,0:T(8,128)(2,1)} %pad_maximum_fusion), channel_id=1, source_target_pairs={{0,4},{4,8},{8,12},{12,16},{16,20},{20,24},{24,28},{28,32},{32,36}... | collective-permute-start | bytes 1572872 | tf_op jit(solution)/shard_map/ppermute | solution.py:16
  36.8 8.4 %copy-start.2 = (bf16[1024,256]{1,0:T(8,128)(2,1)S(1)}, bf16[1024,256]{1,0:T(8,128)(2,1)}, u32[]{:S(2)}) copy-start(bf16[1024,256]{1,0:T(8,128)(2,1)} %get-tuple-element.22) | copy-start | bytes 1572868
  36.8 8.1 %collective-permute-start.2 = (bf16[1024,256]{1,0:T(8,128)(2,1)}, bf16[1024,256]{1,0:T(8,128)(2,1)S(1)}, u32[]{:S(2)}, u32[]{:S(2)}) collective-permute-start(bf16[1024,256]{1,0:T(8,128)(2,1)} %get-tuple-element.22), channel_id=1, source_target_pairs={{0,1},{1,0},{2,3},{3,2},{4,5},{5,4},{6,7},{7,6},{8,9},{9,8},{10,11... | collective-permute-start | bytes 1572872 | tf_op jit(solution)/shard_map/ppermute | solution.py:20
  39.0 5.9 %collective-permute-start.3 = (bf16[256,512]{0,1:T(8,128)(2,1)S(1)}, bf16[256,512]{0,1:T(8,128)(2,1)S(1)}, u32[]{:S(2)}, u32[]{:S(2)}) collective-permute-start(bf16[256,512]{0,1:T(8,128)(2,1)S(1)} %bitcast.35), channel_id=1, source_target_pairs={{0,1},{1,0},{2,3},{3,2},{4,5},{5,4},{6,7},{7,6},{8,9},{9,8},{10,11... | collective-permute-start | bytes 786440 | tf_op jit(solution)/shard_map/ppermute | solution.py:20
  39.2 17.6 %collective-permute-start.6 = (bf16[1024,256]{1,0:T(8,128)(2,1)}, bf16[1024,256]{1,0:T(8,128)(2,1)S(1)}, u32[]{:S(2)}, u32[]{:S(2)}) collective-permute-start(bf16[1024,256]{1,0:T(8,128)(2,1)} %get-tuple-element.29.ret), channel_id=1, source_target_pairs={{0,4},{4,8},{8,12},{12,16},{16,20},{20,24},{24,28},{28,32},{32,36}... | collective-permute-start | bytes 1572872 | tf_op jit(solution)/shard_map/ppermute | solution.py:16
  39.2 17.5 %collective-permute-start.5 = (bf16[1024,256]{1,0:T(8,128)(2,1)}, bf16[1024,256]{1,0:T(8,128)(2,1)S(1)}, u32[]{:S(2)}, u32[]{:S(2)}) collective-permute-start(bf16[1024,256]{1,0:T(8,128)(2,1)} %get-tuple-element.30), channel_id=1, source_target_pairs={{0,124},{4,0},{8,4},{12,8},{16,12},{20,16},{24,20},{28,24},{32,28}... | collective-permute-start | bytes 1572872 | tf_op jit(solution)/shard_map/ppermute | solution.py:16
  46.4 26.8 %collective-permute-start.4 = (bf16[1024,256]{1,0:T(8,128)(2,1)}, bf16[1024,256]{1,0:T(8,128)(2,1)}, u32[]{:S(2)}, u32[]{:S(2)}) collective-permute-start(bf16[1024,256]{1,0:T(8,128)(2,1)} %fusion.2), channel_id=1, source_target_pairs={{0,2},{2,0},{1,3},{3,1},{4,6},{6,4},{5,7},{7,5},{8,10},{10,8},{9,1... | collective-permute-start | bytes 1572872 | tf_op jit(solution)/shard_map/ppermute | solution.py:24
  52.2 20.3 %all-to-all-start = ((bf16[32,32,256]{2,1,0:T(8,128)(2,1)}), bf16[32,32,256]{2,1,0:T(8,128)(2,1)S(1)}, u32[]{:S(2)}, u32[]{:S(2)}) async-start(bf16[32,32,256]{2,1,0:T(8,128)(2,1)} %bitcast.32), calls=%async_computation | async-start | bytes 1048576 | tf_op jit(solution)/shard_map/all_to_all | solution.py:377
  56.8 0.8 %copy-start.3 = (bf16[1024,256]{1,0:T(8,128)(2,1)}, bf16[1024,256]{1,0:T(8,128)(2,1)S(1)}, u32[]{:S(2)}) copy-start(bf16[1024,256]{1,0:T(8,128)(2,1)S(1)} %collective-permute-done.6.high) | copy-start | bytes 1572868
  56.8 1.0 %copy-start.4 = (bf16[1024,256]{1,0:T(8,128)(2,1)}, bf16[1024,256]{1,0:T(8,128)(2,1)S(1)}, u32[]{:S(2)}) copy-start(bf16[1024,256]{1,0:T(8,128)(2,1)S(1)} %collective-permute-done.5.low) | copy-start | bytes 1572868
